TPU v7x, 128 devices: a whole 4x4x4 slice. The times are simulated.
128 devices in a mesh: cfg: 2 (over z_lo), req: 8 (over z_hi, x), seq: 8 (over y, core).
Axes of the slice: x: 4, y: 4, z: 4 (z_hi: 2, z_lo: 2; z = z_hi * 2 + z_lo), core: 2. Of those that a mesh axis runs over, the one named last changes fastest.
Arguments:
- img_state: bfloat16 [2, 16, 1024, 1536], P('cfg', 'req', 'seq'), may hold values from -6 to 6
- txt_state: bfloat16 [2, 16, 192, 1536], P('cfg', 'req', 'seq'), may hold values from -6 to 6
- cond_vec: float32 [2, 16, 1536], P('cfg'), may hold values from -6 to 6
- text_len: int32 [2, 16], P('cfg', 'req'), may hold values from 38 to 154, as said below
- latent: float32 [16, 1024, 64], P('req', 'seq', 'cfg'), may hold values from -6 to 6
- w_mod: bfloat16 [15360, 1536], P(('req', 'seq')), may hold values from -0.15625 to 0.15625
- w_qkv_img: bfloat16 [3, 1536, 1536], P(None, 'seq')
- w_qkv_txt: bfloat16 [3, 1536, 1536], P(None, 'seq')
- w_attn_out: bfloat16 [1536, 1536], P('seq'), may hold values from -2 to 2
- w_up: bfloat16 [6144, 1536], P(('cfg', 'req', 'seq')), may hold values from -0.15625 to 0.15625
- w_down: bfloat16 [6144, 1536], P(('cfg', 'req', 'seq')), may hold values from -0.078125 to 0.078125
- w_final: bfloat16 [1536, 64], replicated, may hold values from -0.078125 to 0.078125
Outputs:
- velocity: float32 [16, 1024, 64], P('req', 'seq', 'cfg')
- latent_next: float32 [16, 1024, 64], P('req', 'seq', 'cfg')
Inputs may be any that keep to these rules, and one draw needn't show every extreme that they name: Text slot t of prompt p in branch c is live when t < text_len[c, p]; every draw has a length equal to 154.
All inputs are finite; a program needn't handle non-finite values.
Results may differ from a plain program's by a relative error of at most 0.02.
Values may be sent and summed in bfloat16 or wider, within the bound.
No kernel may reach another device: no remote copies, remote signals or barrier semaphores. Data moves between devices by JAX's collectives and lax.ppermute only.
A program may use at most 128 MiB of HBM per device.

v0:
```python
import functools
import math

import jax
import jax.numpy as jnp
import numpy as np
from jax import lax
from jax.experimental import pallas as pl
from jax.experimental.pallas import tpu as pltpu
from jax.sharding import Mesh
from jax.sharding import PartitionSpec as P

HEAD = 64
SEQ = ("y", "core")
REQ = ("zhi", "x")
NT = (((1,), (1,)), ((), ()))
NN = (((1,), (0,)), ((), ()))
TN = (((0,), (0,)), ((), ()))
TXT_PAD = 32


def dot(a, b, dims):
    return lax.dot_general(a, b, dims, preferred_element_type=jnp.float32)


def layer_norm(value):
    mean = jnp.mean(value, axis=-1, keepdims=True)
    centered = value - mean
    spread = jnp.mean(centered * centered, axis=-1, keepdims=True)
    return centered * lax.rsqrt(spread + 1e-06)


def attn_kernel(prompt, many, idx_ref, *refs):
    pieces = refs[:many]
    mod_ref, bias_ref, wi_ref, wt_ref, out_ref, x_s, wi_s, wt_s, ai, at, k_s, v_s, q_s, x_sem, w_sem = refs[many:]
    block = x_s.shape[1]
    rows = block - TXT_PAD
    img = many * rows
    keys = many * block
    width = wt_s.shape[0] // 2
    heads = width // HEAD

    def take(s):
        piece = pieces[s] if len(pieces[s].shape) == 2 else pieces[s].at[prompt]
        return pltpu.make_async_copy(piece, x_s.at[s], x_sem.at[s])

    order = [(wi_ref, 0, wi_s, 0), (wi_ref, 2, wi_s, 1), (wi_ref, 1, wi_s, 2), (wt_ref, 2, wt_s, 0), (wt_ref, 1, wt_s, 1)]
    loads = [take(s) for s in range(many)] + [
        pltpu.make_async_copy(src.at[j], dst.at[pl.ds(i * width, width)], w_sem.at[n])
        for n, (src, j, dst, i) in enumerate(order)
    ]
    ahead = 3
    for load in loads[:ahead]:
        load.start()

    def modulated(part, scale, shift):
        normed = layer_norm(part.astype(jnp.float32))
        return (normed * (1.0 + mod_ref[0, scale : scale + 1, :]) + mod_ref[0, shift : shift + 1, :]).astype(
            jnp.bfloat16
        )

    def one_piece(s, carry):
        for n in range(many):

            @pl.when(s == n)
            def _(n=n):
                loads[n].wait()
                loads[n + ahead].start()

        ai[pl.ds(pl.multiple_of(s * rows, rows), rows), :] = modulated(x_s[s, 0:rows, :], 1, 0)
        at[pl.ds(pl.multiple_of(s * TXT_PAD, TXT_PAD), TXT_PAD), :] = modulated(x_s[s, rows:block, :], 7, 6)
        return carry

    lax.fori_loop(0, many, one_piece, 0)
    for load in loads[many + ahead :]:
        load.start()
    for load in loads[many:]:
        load.wait()
    ones = jnp.ones((16, keys), jnp.bfloat16)
    for h in range(heads):
        v_s[h, HEAD : HEAD + 16, :] = ones
        if h:
            q_s[h, 0 : h * HEAD, :] = jnp.zeros((h * HEAD, img), jnp.bfloat16)
        if h + 1 < heads:
            q_s[h, (h + 1) * HEAD :, :] = jnp.zeros((width - (h + 1) * HEAD, img), jnp.bfloat16)
    wide = 2 * rows

    def some_rows(c, carry):
        span = pl.ds(pl.multiple_of(c * wide, wide), wide)
        a = ai[span, :]
        k_s[span, :] = dot(a, wi_s[2 * width : 3 * width, :], NT).astype(jnp.bfloat16)
        both = dot(wi_s[0 : 2 * width, :], a, NT)
        query = (both[0:width] * (HEAD ** (-0.5) * math.log2(math.e))).astype(jnp.bfloat16)
        for h in range(heads):
            q_s[h, h * HEAD : (h + 1) * HEAD, span] = query[h * HEAD : (h + 1) * HEAD]
            v_s[h, 0:HEAD, span] = both[width + h * HEAD : width + (h + 1) * HEAD].astype(jnp.bfloat16)
        return carry

    lax.fori_loop(0, img // wide, some_rows, 0)
    a_txt = at[...]
    k_s[img:keys, :] = dot(a_txt, wt_s[width : 2 * width, :], NT).astype(jnp.bfloat16)
    v_txt = dot(wt_s[0:width, :], a_txt, NT).astype(jnp.bfloat16)
    for h in range(heads):
        v_s[h, 0:HEAD, img:keys] = v_txt[h * HEAD : (h + 1) * HEAD, :]

    def one_head(h, carry):
        query = q_s[h]
        s_img = dot(k_s[0:img, :], query, NN)
        s_txt = dot(k_s[img:keys, :], query, NN) + bias_ref[0]
        top = jnp.maximum(jnp.max(s_img, axis=0, keepdims=True), jnp.max(s_txt, axis=0, keepdims=True))
        p_img = jnp.exp2(s_img - top).astype(jnp.bfloat16)
        p_txt = jnp.exp2(s_txt - top).astype(jnp.bfloat16)
        o = dot(v_s[h, :, 0:img], p_img, NN) + dot(v_s[h, :, img:keys], p_txt, NN)
        o = (o[0:HEAD] / o[HEAD : HEAD + 1]).astype(jnp.bfloat16)
        for i in range(many):
            out_ref[idx_ref[i], pl.ds(pl.multiple_of(h * HEAD, HEAD), HEAD), :] = o[:, i * rows : (i + 1) * rows]
        return carry

    lax.fori_loop(0, heads, one_head, 0)


def attention(prompt, owners, pieces, mod, bias, w_img, w_txt):
    many = len(pieces)
    block, depth = pieces[0].shape[-2:]
    rows = block - TXT_PAD
    width = w_img.shape[1]
    heads = width // HEAD
    keys = many * block
    once = lambda *zeros: (lambda i, owners: zeros)
    stays = pl.BlockSpec(memory_space=pltpu.HBM)
    bf16 = jnp.bfloat16
    return pl.pallas_call(
        functools.partial(attn_kernel, prompt, many),
        out_shape=jax.ShapeDtypeStruct((many, width, rows), bf16),
        grid_spec=pltpu.PrefetchScalarGridSpec(
            num_scalar_prefetch=1,
            grid=(1,),
            in_specs=[stays] * many
            + [
                pl.BlockSpec((1, 10, depth), once(prompt, 0, 0)),
                pl.BlockSpec((1, many * TXT_PAD, 1), once(prompt, 0, 0)),
                stays,
                stays,
            ],
            out_specs=pl.BlockSpec((many, width, rows), once(0, 0, 0)),
            scratch_shapes=[
                pltpu.VMEM((many, block, depth), bf16),
                pltpu.VMEM((3 * width, depth), bf16),
                pltpu.VMEM((2 * width, depth), bf16),
                pltpu.VMEM((many * rows, depth), bf16),
                pltpu.VMEM((many * TXT_PAD, depth), bf16),
                pltpu.VMEM((keys, width), bf16),
                pltpu.VMEM((heads, HEAD + 16, keys), bf16),
                pltpu.VMEM((heads, width, many * rows), bf16),
                pltpu.SemaphoreType.DMA((many,)),
                pltpu.SemaphoreType.DMA((5,)),
            ],
        ),
        compiler_params=pltpu.CompilerParams(vmem_limit_bytes=56 << 20),
        cost_estimate=pl.CostEstimate(flops=8000000000, bytes_accessed=8000000, transcendentals=0),
        name="attn",
    )(owners, *pieces, mod, bias, w_img, w_txt)


def proj_kernel(many, prompts, idx_ref, *refs):
    atts, parts = refs[:prompts], refs[prompts : prompts + many]
    img_ref, mod_ref, resid_ref, normed_ref, w_s, att_s, sem = refs[prompts + many :]
    rows = img_ref.shape[2]
    loads, owner, at = [], [], 0
    size = parts[0].shape[0]
    for n, part in enumerate(parts):
        loads.append(pltpu.make_async_copy(part, w_s.at[pl.ds(at, part.shape[0])], sem.at[n]))
        at += part.shape[0]
    for load in loads:
        load.start()
    for p, att in enumerate(atts):
        for s in range(w_s.shape[0] // size):
            att_s[s * size : (s + 1) * size, p * rows : (p + 1) * rows] = att[idx_ref[s]]
    for load in loads:
        load.wait()
    total = dot(att_s[...], w_s[...], TN)
    for p in range(prompts):
        span = slice(p * rows, (p + 1) * rows)
        one = (img_ref[0, p].astype(jnp.float32) + mod_ref[p, 2:3, :] * total[span]).astype(jnp.bfloat16)
        resid_ref[span, :] = one
        normed = layer_norm(one.astype(jnp.float32)) * (1.0 + mod_ref[p, 4:5, :]) + mod_ref[p, 3:4, :]
        normed_ref[span, :] = normed.astype(jnp.bfloat16)


def project(owners, atts, parts, img_state, mod):
    prompts, rows, depth = img_state.shape[1:]
    many = len(parts)
    total = sum(part.shape[0] for part in parts)
    once = lambda *zeros: (lambda i, owners: zeros)
    return pl.pallas_call(
        functools.partial(proj_kernel, many, prompts),
        out_shape=[jax.ShapeDtypeStruct((prompts * rows, depth), jnp.bfloat16)] * 2,
        grid_spec=pltpu.PrefetchScalarGridSpec(
            num_scalar_prefetch=1,
            grid=(1,),
            in_specs=[pl.BlockSpec(att.shape, once(0, 0, 0)) for att in atts]
            + [pl.BlockSpec(memory_space=pltpu.HBM)] * many
            + [
                pl.BlockSpec((1, prompts, rows, depth), once(0, 0, 0, 0)),
                pl.BlockSpec((prompts, 10, depth), once(0, 0, 0)),
            ],
            out_specs=[pl.BlockSpec((prompts * rows, depth), once(0, 0))] * 2,
            scratch_shapes=[
                pltpu.VMEM((total, depth), jnp.bfloat16),
                pltpu.VMEM((total, prompts * rows), jnp.bfloat16),
                pltpu.SemaphoreType.DMA((many,)),
            ],
        ),
        compiler_params=pltpu.CompilerParams(vmem_limit_bytes=56 << 20),
        cost_estimate=pl.CostEstimate(flops=1200000000, bytes_accessed=5000000, transcendentals=0),
        name="proj",
    )(owners, *atts, *parts, img_state, mod)


def mlp_kernel(many, *refs):
    pieces, w_ref = refs[:many], refs[many]
    *outs, x_s, up_s, down_s, hid_s, sem = refs[many + 1 :]
    shards, units, depth = up_s.shape
    group = 8
    chunks = shards // group
    chunk = group * units

    def load(half, dst, c):
        span = pl.ds(c * group, group)
        return pltpu.make_async_copy(w_ref.at[span, half], dst.at[span], sem.at[half * chunks + c])

    load(0, up_s, 0).start()
    load(0, up_s, 1).start()
    at = 0
    for piece in pieces:
        x_s[at : at + piece.shape[0], :] = piece[...]
        at += piece.shape[0]

    def one_chunk(c, carry):
        load(0, up_s, c).wait()

        @pl.when(c + 2 < chunks)
        def _():
            load(0, up_s, c + 2).start()

        @pl.when(c + 2 >= chunks)
        def _():
            load(1, down_s, c + 2 - chunks).start()

        up = up_s[pl.ds(c * group, group)].reshape(chunk, depth)
        inner = jax.nn.gelu(dot(x_s[...], up, NT), approximate=True)
        hid_s[:, pl.ds(pl.multiple_of(c * chunk, chunk), chunk)] = inner.astype(jnp.bfloat16)
        return carry

    lax.fori_loop(0, chunks, one_chunk, 0)
    for c in range(2, chunks):
        load(1, down_s, c).start()
    for c in range(chunks):
        load(1, down_s, c).wait()
    wide = 512
    rows = outs[0].shape[0]

    def some_columns(n, carry):
        span = pl.ds(pl.multiple_of(n * wide, wide), wide)
        down = down_s[:, :, span].reshape(chunks * chunk, wide)
        total = dot(hid_s[...], down, NN)
        for i, out in enumerate(outs):
            out[:, span] = total[i * rows : (i + 1) * rows].astype(out.dtype)
        return carry

    lax.fori_loop(0, depth // wide, some_columns, 0)


def mlp(pieces, types, weights):
    shards, _, units, width = weights.shape
    many = len(pieces)
    count = sum(piece.shape[0] for piece in pieces)
    rows = count // len(types)
    return pl.pallas_call(
        functools.partial(mlp_kernel, many),
        out_shape=[jax.ShapeDtypeStruct((rows, width), t) for t in types],
        grid=(1,),
        in_specs=[pl.BlockSpec(piece.shape, lambda i: (0, 0)) for piece in pieces]
        + [pl.BlockSpec(memory_space=pltpu.HBM)],
        out_specs=[pl.BlockSpec((rows, width), lambda i: (0, 0))] * len(types),
        scratch_shapes=[
            pltpu.VMEM((count, width), jnp.bfloat16),
            pltpu.VMEM((shards, units, width), jnp.bfloat16),
            pltpu.VMEM((shards, units, width), jnp.bfloat16),
            pltpu.VMEM((count, shards * units), jnp.bfloat16),
            pltpu.SemaphoreType.DMA((shards // 4,)),
        ],
        compiler_params=pltpu.CompilerParams(vmem_limit_bytes=56 << 20),
        cost_estimate=pl.CostEstimate(
            flops=4 * count * shards * units * width,
            bytes_accessed=4 * shards * units * width,
            transcendentals=0,
        ),
        name="mlp",
    )(*pieces, weights)


def finish_kernel(mod_ref, w_ref, resid_ref, own_ref, *refs):
    *terms, mine_ref, others_ref = refs
    prompts, half, rows = mine_ref.shape
    for p in range(prompts):
        span = slice(p * rows, (p + 1) * rows)
        total = own_ref[span, :]
        for term in terms[2 * p : 2 * p + 2]:
            total = total + term[...].astype(jnp.float32)
        two = resid_ref[span, :].astype(jnp.float32) + mod_ref[p, 5:6, :] * total
        last = layer_norm(two) * (1.0 + mod_ref[p, 9:10, :]) + mod_ref[p, 8:9, :]
        vel = dot(w_ref[...], last.astype(jnp.bfloat16), (((0,), (1,)), ((), ())))
        mine_ref[p] = vel[0:half]
        others_ref[p] = vel[half:].astype(jnp.bfloat16)


def finish(resid, own, terms, mod, w_last):
    prompts = mod.shape[0]
    half = w_last.shape[1] // 2
    shape = (prompts, half, resid.shape[0] // prompts)
    return pl.pallas_call(
        finish_kernel,
        out_shape=[jax.ShapeDtypeStruct(shape, jnp.float32), jax.ShapeDtypeStruct(shape, jnp.bfloat16)],
        compiler_params=pltpu.CompilerParams(vmem_limit_bytes=32 << 20),
        name="finish",
    )(mod, w_last, resid, own, *terms)


def shifted(value, axis, by):
    size = lax.axis_size(axis)
    return lax.ppermute(value, axis, [(i, (i + by) % size) for i in range(size)])


def swap(value, axis):
    return shifted(value, axis, 1)


def along_z(value, by):
    place = lambda z: z % 2 * 2 + z // 2
    pairs = [(place(z), place((z + by) % 4)) for z in range(4)]
    return lax.ppermute(value, ("cfg", "zhi"), pairs)


def local(
    img_state,
    txt_state,
    cond_vec,
    text_len,
    latent,
    w_mod,
    w_qkv_img,
    w_qkv_txt,
    w_attn_out,
    w_up,
    w_down,
    w_final,
):
    prompts = img_state.shape[1]
    rows = img_state.shape[2]
    width = img_state.shape[3]
    txt_rows = txt_state.shape[2]
    high = lax.axis_size("y")
    seqs = high * lax.axis_size("core")
    reqs = lax.axis_size("zhi") * lax.axis_size("x")
    everyone = reqs * seqs

    padding = jnp.zeros((TXT_PAD - txt_rows, width), jnp.bfloat16)
    tokens, before = [], None
    for p in range(prompts):
        mine = jnp.concatenate([img_state[0, p], txt_state[0, p], padding], axis=0)
        if before is not None:
            mine, *before = lax.optimization_barrier((mine, *before))
        below, above = shifted(mine, "y", 1), shifted(mine, "y", -1)
        before = [below, above]
        far = shifted(below, "y", 1) if p % 2 == 0 else shifted(above, "y", -1)
        same = [mine, below, above, far]
        tokens.append(same + [swap(block, "core") for block in same])

    weights = lax.all_gather(
        jnp.stack([w_up, w_down])[None], ("x",) + SEQ, axis=0, tiled=True
    )

    cond_act = jax.nn.silu(cond_vec[0]).astype(jnp.bfloat16)
    part = dot(cond_act, w_mod, NT)
    cols = part.shape[1]
    lanes = -(-cols // 128) * 128
    part = jnp.pad(part, ((0, 0), (0, lanes - cols)))
    part = part.reshape(reqs, 1, prompts * lanes // 128, 128)
    part = jnp.broadcast_to(part, (reqs, seqs) + part.shape[2:]).reshape((everyone,) + part.shape[2:])
    got = lax.all_to_all(part, REQ + SEQ, 0, 0, tiled=True)
    got = got.reshape(everyone, prompts, lanes)[:, :, :cols]
    mod = jnp.swapaxes(got, 0, 1).reshape(prompts, 10, width)

    here, core = lax.axis_index("y"), lax.axis_index("core")
    level = (here + jnp.array([0, high - 1, 1, 2], jnp.int32)) % high
    owners = jnp.concatenate([2 * level + core, 2 * level + 1 - core]).astype(jnp.int32)
    inside = jnp.arange(TXT_PAD)
    index = owners[:, None] * txt_rows + inside[None, :]
    live = (inside < txt_rows)[None, None, :] & (index[None] < text_len[0][:, None, None])
    bias = jnp.where(live, 0.0, -1e30).astype(jnp.float32).reshape(prompts, seqs * TXT_PAD, 1)

    att = [
        attention(p, owners, tokens[p], mod, bias, w_qkv_img, w_qkv_txt) for p in range(prompts)
    ]
    late, _ = lax.optimization_barrier((w_attn_out, far))
    below, above = shifted(late, "y", 1), shifted(late, "y", -1)
    last = att[-1]
    att = [lax.all_to_all(a, SEQ, 0, 0, tiled=True) for a in att]
    below, above, last = lax.optimization_barrier((below, above, last))
    cut = late.shape[0] // 2
    far = [shifted(below[:cut], "y", 1), shifted(above[cut:], "y", -1)]
    parts = [late, below, above] + far
    parts = parts + [swap(part, "core") for part in parts]
    resid, normed = project(owners, att, parts, img_state, mod)
    f32, bf16 = jnp.float32, jnp.bfloat16
    low, high_rows = along_z(normed, 1), along_z(normed, -1)
    away = [along_z(low[:rows], 1), along_z(high_rows[rows:], -1)]
    (own,) = mlp([normed], [f32], weights)
    low, high_rows, before = lax.optimization_barrier((low, high_rows, own))
    low0, low1, high0, high1 = mlp([low, high_rows], [bf16, f32, f32, bf16], weights)
    away, before = lax.optimization_barrier((away, low0))
    hop0, hop1 = mlp(away, [bf16, bf16], weights)
    hop0, hop1 = along_z(hop0, 1), along_z(hop1, -1)
    terms = [along_z(low0, -1), along_z((high0 + hop0.astype(f32)).astype(bf16), 1)]
    terms += [along_z(high1, 1), along_z((low1 + hop1.astype(f32)).astype(bf16), -1)]

    half = latent.shape[2]
    branch = lax.axis_index("cfg")
    first = branch == 0
    w_last = jnp.where(first, w_final, jnp.concatenate([w_final[:, half:], w_final[:, :half]], axis=1))
    mine, others = finish(resid, own, terms, mod, w_last)
    partner = swap(others, "cfg").astype(jnp.float32)
    cond_vel = jnp.where(first, mine, partner)
    uncond_vel = jnp.where(first, partner, mine)
    velocity = uncond_vel + 4.5 * (cond_vel - uncond_vel)
    latent_next = jnp.swapaxes(latent, 1, 2) - 0.04 * velocity
    return jnp.swapaxes(velocity, 1, 2), jnp.swapaxes(latent_next, 1, 2)


def solution(mesh):
    fine = Mesh(np.asarray(mesh.devices).reshape(2, 2, 4, 4, 2), ("cfg", "zhi", "x", "y", "core"))
    every = ("cfg",) + REQ + SEQ
    placed = (
        P("cfg", REQ, SEQ, None),
        P("cfg", REQ, SEQ, None),
        P("cfg", None, None),
        P("cfg", REQ),
        P(REQ, SEQ, "cfg"),
        P(REQ + SEQ, None),
        P(None, SEQ, None),
        P(None, SEQ, None),
        P(SEQ, None),
        P(every, None),
        P(every, None),
        P(),
    )
    return jax.shard_map(
        local,
        mesh=fine,
        in_specs=placed,
        out_specs=(P(REQ, SEQ, "cfg"), P(REQ, SEQ, "cfg")),
        check_vma=False,
    )
```

profile of v0, /device:TPU:70, one launch (start us, length us, event | category | flops | bytes accessed | tf_op | source)
XLA Modules:
  0.0 251.6 jit_solution(6295974364429792881)
XLA Ops:
  15.0 11.0 %collective-permute-done.refs_1_ = bf16[160,1536]{1,0:T(8,128)(2,1)S(1)} collective-permute-done((bf16[160,1536]{1,0:T(8,128)(2,1)S(1)}, bf16[160,1536]{1,0:T(8,128)(2,1)S(1)}, u32[]{:S(2)}, u32[]{:S(2)}) %collective-permute-start) | collective-permute-done | bytes 491552 | tf_op jit(solution)/shard_map/ppermute | solution.py:332
  27.7 3.1 %collective-permute-start.8 = (bf16[160,1536]{1,0:T(8,128)(2,1)S(1)}, bf16[160,1536]{1,0:T(8,128)(2,1)}, u32[]{:S(2)}, u32[]{:S(2)}) collective-permute-start(bf16[160,1536]{1,0:T(8,128)(2,1)S(1)} %get-tuple-element.20.refs_0_), channel_id=1, source_target_pairs={{0,6},{2,0},{4,2},{6,4},{1,7},{3,1},{5,3},{7,5},{8,14},{10,8},{12,... | collective-permute-start | bytes 1474568 | tf_op jit(solution)/shard_map/ppermute | solution.py:332
  31.7 8.3 %all-to-all-start = ((f32[64,4,128]{2,1,0:T(4,128)}), f32[64,4,128]{2,1,0:T(4,128)S(1)}, u32[]{:S(2)}, u32[]{:S(2)}) async-start(f32[64,4,128]{2,1,0:T(4,128)} %bitcast.1), calls=%async_computation | async-start | bytes 262144 | tf_op jit(solution)/shard_map/all_to_all | solution.py:391
  42.0 4.1 %collective-permute-start.9 = (bf16[160,1536]{1,0:T(8,128)(2,1)}, bf16[160,1536]{1,0:T(8,128)(2,1)S(1)}, u32[]{:S(2)}, u32[]{:S(2)}) collective-permute-start(bf16[160,1536]{1,0:T(8,128)(2,1)} %collective-permute-done.8.refs_2_), channel_id=1, source_target_pairs={{0,6},{2,0},{4,2},{6,4},{1,7},{3,1},{5,3},{7,5},{8,14},{10,8},{12,... | collective-permute-start | bytes 1474568 | tf_op jit(solution)/shard_map/ppermute | solution.py:332
  46.9 17.2 %collective-permute-done.2.refs_3_ = bf16[160,1536]{1,0:T(8,128)(2,1)} collective-permute-done((bf16[160,1536]{1,0:T(8,128)(2,1)S(1)}, bf16[160,1536]{1,0:T(8,128)(2,1)}, u32[]{:S(2)}, u32[]{:S(2)}) %collective-permute-start.2) | collective-permute-done | bytes 491552 | tf_op jit(solution)/shard_map/ppermute | solution.py:332
  69.9 15.1 %collective-permute-done.7.refs_1_ = bf16[160,1536]{1,0:T(8,128)(2,1)} collective-permute-done((bf16[160,1536]{1,0:T(8,128)(2,1)S(1)}, bf16[160,1536]{1,0:T(8,128)(2,1)}, u32[]{:S(2)}, u32[]{:S(2)}) %collective-permute-start.7) | collective-permute-done | bytes 491552 | tf_op jit(solution)/shard_map/ppermute | solution.py:332
  85.7 16.9 %attn.2 = bf16[8,192,128]{2,1,0:T(8,128)(2,1)} custom-call(s32[8]{0:T(128)} %get-tuple-element.39.idx_ref, bf16[160,1536]{1,0:T(8,128)(2,1)} %copy-done.12, bf16[160,1536]{1,0:T(8,128)(2,1)} %copy-done.20, bf16[160,1536]{1,0:T(8,128)(2,1)} %collective-permute-done.1.refs_2_, bf16[160,1536]{1,0:T(8,128)(2,1)} %collective-permute-done.2.refs_3_, ...), custom_call_target="tpu_custom_call" | custom-call | flops 8000000000 | bytes 8000000 | tf_op jit(solution)/shard_map/attn/pallas_call | solution.py:132
  102.7 4.5 %all-to-all-start.1 = ((bf16[8,192,128]{2,1,0:T(8,128)(2,1)}), bf16[8,192,128]{2,1,0:T(8,128)(2,1)S(1)}, u32[]{:S(2)}, u32[]{:S(2)}) async-start(bf16[8,192,128]{2,1,0:T(8,128)(2,1)} %attn.2), calls=%async_computation.1 | async-start | bytes 786432 | tf_op jit(solution)/shard_map/all_to_all | solution.py:409
  107.1 3.2 %collective-permute-start.15 = (bf16[192,1536]{1,0:T(8,128)(2,1)S(1)}, bf16[192,1536]{1,0:T(8,128)(2,1)S(1)}, u32[]{:S(2)}, u32[]{:S(2)}) collective-permute-start(bf16[192,1536]{1,0:T(8,128)(2,1)S(1)} %copy-done.10), channel_id=1, source_target_pairs={{0,6},{2,0},{4,2},{6,4},{1,7},{3,1},{5,3},{7,5},{8,14},{10,8},{12,... | collective-permute-start | bytes 1769480 | tf_op jit(solution)/shard_map/ppermute | solution.py:332
  110.4 17.0 %attn.3 = bf16[8,192,128]{2,1,0:T(8,128)(2,1)} custom-call(s32[8]{0:T(128)} %get-tuple-element.39.idx_ref, bf16[160,1536]{1,0:T(8,128)(2,1)} %copy-done.11, bf16[160,1536]{1,0:T(8,128)(2,1)} %collective-permute-done.7.refs_1_, bf16[160,1536]{1,0:T(8,128)(2,1)} %collective-permute-done.8.refs_2_, bf16[160,1536]{1,0:T(8,128)(2,1)} %copy-done.21, ...), custom_call_target="tpu_custom_call" | custom-call | flops 8000000000 | bytes 8000000 | tf_op jit(solution)/shard_map/attn/pallas_call | solution.py:132
  132.7 3.5 %all-to-all-start.2 = ((bf16[8,192,128]{2,1,0:T(8,128)(2,1)}), bf16[8,192,128]{2,1,0:T(8,128)(2,1)S(1)}, u32[]{:S(2)}, u32[]{:S(2)}) async-start(bf16[8,192,128]{2,1,0:T(8,128)(2,1)} %attn.3), calls=%async_computation.2 | async-start | bytes 786432 | tf_op jit(solution)/shard_map/all_to_all | solution.py:409
  136.1 3.0 %collective-permute-done.16.refs_5_ = bf16[96,1536]{1,0:T(8,128)(2,1)} collective-permute-done((bf16[96,1536]{1,0:T(8,128)(2,1)}, bf16[96,1536]{1,0:T(8,128)(2,1)}, u32[]{:S(2)}, u32[]{:S(2)}) %collective-permute-start.16) | collective-permute-done | bytes 294944 | tf_op jit(solution)/shard_map/ppermute | solution.py:332
  140.2 4.8 %all-to-all-done.2.refs_1_ = bf16[8,192,128]{2,1,0:T(8,128)(2,1)S(1)} async-done(((bf16[8,192,128]{2,1,0:T(8,128)(2,1)}), bf16[8,192,128]{2,1,0:T(8,128)(2,1)S(1)}, u32[]{:S(2)}, u32[]{:S(2)}) %all-to-all-start.2) | async-done | bytes 393248 | tf_op jit(solution)/shard_map/all_to_all | solution.py:409
  145.8 7.3 %proj.1 = (bf16[256,1536]{1,0:T(8,128)(2,1)}, bf16[256,1536]{1,0:T(8,128)(2,1)}) custom-call(s32[8]{0:T(128)} %get-tuple-element.39.idx_ref, bf16[8,192,128]{2,1,0:T(8,128)(2,1)} %copy-done.4, bf16[8,192,128]{2,1,0:T(8,128)(2,1)} %copy-done.5, bf16[192,1536]{1,0:T(8,128)(2,1)} %refs_2_, bf16[192,1536]{1,0:T(8,128)(2,1)} %copy-done.6, ...), custom_call_target="tpu_custom_call" | custom-call | flops 1200000000 | bytes 5000000 | tf_op jit(solution)/shard_map/proj/pallas_call | solution.py:195
  156.3 16.1 %collective-permute-done.23.refs_0_ = bf16[256,1536]{1,0:T(8,128)(2,1)S(1)} collective-permute-done((bf16[256,1536]{1,0:T(8,128)(2,1)}, bf16[256,1536]{1,0:T(8,128)(2,1)S(1)}, u32[]{:S(2)}, u32[]{:S(2)}) %collective-permute-start.23) | collective-permute-done | bytes 786464 | tf_op jit(solution)/shard_map/ppermute | solution.py:342
  175.7 9.5 %mlp.3.own_ref = f32[256,1536]{1,0:T(8,128)} custom-call(bf16[256,1536]{1,0:T(8,128)(2,1)} %get-tuple-element.25.refs_0_, bf16[32,2,48,1536]{3,2,1,0:T(8,128)(2,1)} %bitcast.38), custom_call_target="tpu_custom_call" | custom-call | flops 2415919104 | bytes 9437184 | tf_op jit(solution)/shard_map/mlp/pallas_call | solution.py:279
  185.2 13.0 %mlp.4 = (bf16[128,1536]{1,0:T(8,128)(2,1)}, f32[128,1536]{1,0:T(8,128)}, f32[128,1536]{1,0:T(8,128)}, bf16[128,1536]{1,0:T(8,128)(2,1)}) custom-call(bf16[256,1536]{1,0:T(8,128)(2,1)} %copy-done.15, bf16[256,1536]{1,0:T(8,128)(2,1)} %collective-permute-done.24.refs_1_, bf16[32,2,48,1536]{3,2,1,0:T(8,128)(2,1)} %bitcast.39), custom_call_target="tpu_custom_call" | custom-call | flops 4831838208 | bytes 9437184 | tf_op jit(solution)/shard_map/mlp/pallas_call | solution.py:279
  199.2 9.6 %mlp.5 = (bf16[128,1536]{1,0:T(8,128)(2,1)}, bf16[128,1536]{1,0:T(8,128)(2,1)}) custom-call(bf16[128,1536]{1,0:T(8,128)(2,1)} %copy-done.13, bf16[128,1536]{1,0:T(8,128)(2,1)} %copy-done.14, bf16[32,2,48,1536]{3,2,1,0:T(8,128)(2,1)} %bitcast.40), custom_call_target="tpu_custom_call" | custom-call | flops 2415919104 | bytes 9437184 | tf_op jit(solution)/shard_map/mlp/pallas_call | solution.py:279
  210.1 3.1 %collective-permute-start.25 = (bf16[128,1536]{1,0:T(8,128)(2,1)S(1)}, bf16[128,1536]{1,0:T(8,128)(2,1)S(1)}, u32[]{:S(2)}, u32[]{:S(2)}) collective-permute-start(bf16[128,1536]{1,0:T(8,128)(2,1)S(1)} %copy-done.23), channel_id=1, source_target_pairs={{0,96},{64,0},{32,64},{96,32},{1,97},{65,1},{33,65},{97,33},{2,98}... | collective-permute-start | bytes 1179656 | tf_op jit(solution)/shard_map/ppermute | solution.py:342
  214.5 6.7 %collective-permute-done.31 = bf16[128,1536]{1,0:T(8,128)(2,1)S(1)} collective-permute-done((bf16[128,1536]{1,0:T(8,128)(2,1)}, bf16[128,1536]{1,0:T(8,128)(2,1)S(1)}, u32[]{:S(2)}, u32[]{:S(2)}) %collective-permute-start.31) | collective-permute-done | bytes 393248 | tf_op jit(solution)/shard_map/ppermute | solution.py:342
  225.9 3.8 %collective-permute-done.25.refs_0_ = bf16[128,1536]{1,0:T(8,128)(2,1)S(1)} collective-permute-done((bf16[128,1536]{1,0:T(8,128)(2,1)S(1)}, bf16[128,1536]{1,0:T(8,128)(2,1)S(1)}, u32[]{:S(2)}, u32[]{:S(2)}) %collective-permute-start.25) | collective-permute-done | bytes 393248 | tf_op jit(solution)/shard_map/ppermute | solution.py:342
  229.7 4.2 %collective-permute-done.30.refs_2_ = bf16[128,1536]{1,0:T(8,128)(2,1)S(1)} collective-permute-done((bf16[128,1536]{1,0:T(8,128)(2,1)S(1)}, bf16[128,1536]{1,0:T(8,128)(2,1)S(1)}, u32[]{:S(2)}, u32[]{:S(2)}) %collective-permute-start.30) | collective-permute-done | bytes 393248 | tf_op jit(solution)/shard_map/ppermute | solution.py:342
  235.5 3.7 %collective-permute-done.29.refs_1_ = bf16[128,1536]{1,0:T(8,128)(2,1)S(1)} collective-permute-done((bf16[128,1536]{1,0:T(8,128)(2,1)S(1)}, bf16[128,1536]{1,0:T(8,128)(2,1)S(1)}, u32[]{:S(2)}, u32[]{:S(2)}) %collective-permute-start.29) | collective-permute-done | bytes 393248 | tf_op jit(solution)/shard_map/ppermute | solution.py:342
  240.7 3.5 %collective-permute-done.33 = bf16[2,32,128]{2,1,0:T(8,128)(2,1)S(1)} collective-permute-done((bf16[2,32,128]{2,1,0:T(8,128)(2,1)S(1)}, bf16[2,32,128]{2,1,0:T(8,128)(2,1)S(1)}, u32[]{:S(2)}, u32[]{:S(2)}) %collective-permute-start.33) | collective-permute-done | bytes 16416 | tf_op jit(solution)/shard_map/ppermute | solution.py:332
  (144 shorter events, 45.1 us)
Async XLA Ops:
  7.2 168.5 %all-gather.3.cloned.1.call-start = ((), (), s32[]{:S(2)}) async-start(), calls=%async_computation.3 | async-start | bytes 9732096 | tf_op jit(solution)/shard_map/all_gather | solution.py:380
  13.3 14.4 %collective-permute-start.1 = (bf16[160,1536]{1,0:T(8,128)(2,1)S(1)}, bf16[160,1536]{1,0:T(8,128)(2,1)}, u32[]{:S(2)}, u32[]{:S(2)}) collective-permute-start(bf16[160,1536]{1,0:T(8,128)(2,1)S(1)} %get-tuple-element.51.refs_0_), channel_id=1, source_target_pairs={{0,6},{2,0},{4,2},{6,4},{1,7},{3,1},{5,3},{7,5},{8,14},{10,8},{12,... | collective-permute-start | bytes 1474568 | tf_op jit(solution)/shard_map/ppermute | solution.py:332
  30.7 39.2 %collective-permute-start.3 = (bf16[160,1536]{1,0:T(8,128)(2,1)S(1)}, bf16[160,1536]{1,0:T(8,128)(2,1)}, u32[]{:S(2)}, u32[]{:S(2)}) collective-permute-start(bf16[160,1536]{1,0:T(8,128)(2,1)S(1)} %get-tuple-element.51.refs_0_), channel_id=1, source_target_pairs={{0,1},{1,0},{2,3},{3,2},{4,5},{5,4},{6,7},{7,6},{8,9},{9,8},{10,11... | collective-permute-start | bytes 1474568 | tf_op jit(solution)/shard_map/ppermute | solution.py:332
  31.7 37.2 %all-to-all-start = ((f32[64,4,128]{2,1,0:T(4,128)}), f32[64,4,128]{2,1,0:T(4,128)S(1)}, u32[]{:S(2)}, u32[]{:S(2)}) async-start(f32[64,4,128]{2,1,0:T(4,128)} %bitcast.1), calls=%async_computation | async-start | bytes 262144 | tf_op jit(solution)/shard_map/all_to_all | solution.py:391
  40.0 24.1 %collective-permute-start.2 = (bf16[160,1536]{1,0:T(8,128)(2,1)S(1)}, bf16[160,1536]{1,0:T(8,128)(2,1)}, u32[]{:S(2)}, u32[]{:S(2)}) collective-permute-start(bf16[160,1536]{1,0:T(8,128)(2,1)S(1)} %collective-permute-done.refs_1_), channel_id=1, source_target_pairs={{0,2},{2,4},{4,6},{6,0},{1,3},{3,5},{5,7},{7,1},{8,10},{10,12},{12... | collective-permute-start | bytes 1474568 | tf_op jit(solution)/shard_map/ppermute | solution.py:332
  42.0 25.0 %collective-permute-start.9 = (bf16[160,1536]{1,0:T(8,128)(2,1)}, bf16[160,1536]{1,0:T(8,128)(2,1)S(1)}, u32[]{:S(2)}, u32[]{:S(2)}) collective-permute-start(bf16[160,1536]{1,0:T(8,128)(2,1)} %collective-permute-done.8.refs_2_), channel_id=1, source_target_pairs={{0,6},{2,0},{4,2},{6,4},{1,7},{3,1},{5,3},{7,5},{8,14},{10,8},{12,... | collective-permute-start | bytes 1474568 | tf_op jit(solution)/shard_map/ppermute | solution.py:332
  46.8 38.3 %collective-permute-start.7 = (bf16[160,1536]{1,0:T(8,128)(2,1)S(1)}, bf16[160,1536]{1,0:T(8,128)(2,1)}, u32[]{:S(2)}, u32[]{:S(2)}) collective-permute-start(bf16[160,1536]{1,0:T(8,128)(2,1)S(1)} %get-tuple-element.20.refs_0_), channel_id=1, source_target_pairs={{0,2},{2,4},{4,6},{6,0},{1,3},{3,5},{5,7},{7,1},{8,10},{10,12},{12... | collective-permute-start | bytes 1474568 | tf_op jit(solution)/shard_map/ppermute | solution.py:332
  46.8 38.2 %collective-permute-start.4 = (bf16[160,1536]{1,0:T(8,128)(2,1)S(1)}, bf16[160,1536]{1,0:T(8,128)(2,1)}, u32[]{:S(2)}, u32[]{:S(2)}) collective-permute-start(bf16[160,1536]{1,0:T(8,128)(2,1)S(1)} %collective-permute-done.refs_1_), channel_id=1, source_target_pairs={{0,1},{1,0},{2,3},{3,2},{4,5},{5,4},{6,7},{7,6},{8,9},{9,8},{10,11... | collective-permute-start | bytes 1474568 | tf_op jit(solution)/shard_map/ppermute | solution.py:332
  64.1 21.4 %collective-permute-start.5 = (bf16[160,1536]{1,0:T(8,128)(2,1)}, bf16[160,1536]{1,0:T(8,128)(2,1)}, u32[]{:S(2)}, u32[]{:S(2)}) collective-permute-start(bf16[160,1536]{1,0:T(8,128)(2,1)} %collective-permute-done.1.refs_2_), channel_id=1, source_target_pairs={{0,1},{1,0},{2,3},{3,2},{4,5},{5,4},{6,7},{7,6},{8,9},{9,8},{10,11... | collective-permute-start | bytes 1474568 | tf_op jit(solution)/shard_map/ppermute | solution.py:332
  67.0 18.5 %collective-permute-start.6 = (bf16[160,1536]{1,0:T(8,128)(2,1)}, bf16[160,1536]{1,0:T(8,128)(2,1)}, u32[]{:S(2)}, u32[]{:S(2)}) collective-permute-start(bf16[160,1536]{1,0:T(8,128)(2,1)} %collective-permute-done.2.refs_3_), channel_id=1, source_target_pairs={{0,1},{1,0},{2,3},{3,2},{4,5},{5,4},{6,7},{7,6},{8,9},{9,8},{10,11... | collective-permute-start | bytes 1474568 | tf_op jit(solution)/shard_map/ppermute | solution.py:332
  69.9 37.2 %collective-permute-start.10 = (bf16[160,1536]{1,0:T(8,128)(2,1)S(1)}, bf16[160,1536]{1,0:T(8,128)(2,1)}, u32[]{:S(2)}, u32[]{:S(2)}) collective-permute-start(bf16[160,1536]{1,0:T(8,128)(2,1)S(1)} %get-tuple-element.20.refs_0_), channel_id=1, source_target_pairs={{0,1},{1,0},{2,3},{3,2},{4,5},{5,4},{6,7},{7,6},{8,9},{9,8},{10,11... | collective-permute-start | bytes 1474568 | tf_op jit(solution)/shard_map/ppermute | solution.py:332
  85.0 25.3 %collective-permute-start.12 = (bf16[160,1536]{1,0:T(8,128)(2,1)}, bf16[160,1536]{1,0:T(8,128)(2,1)}, u32[]{:S(2)}, u32[]{:S(2)}) collective-permute-start(bf16[160,1536]{1,0:T(8,128)(2,1)} %collective-permute-done.8.refs_2_), channel_id=1, source_target_pairs={{0,1},{1,0},{2,3},{3,2},{4,5},{5,4},{6,7},{7,6},{8,9},{9,8},{10,11... | collective-permute-start | bytes 1474568 | tf_op jit(solution)/shard_map/ppermute | solution.py:332
  85.0 25.3 %collective-permute-start.11 = (bf16[160,1536]{1,0:T(8,128)(2,1)}, bf16[160,1536]{1,0:T(8,128)(2,1)}, u32[]{:S(2)}, u32[]{:S(2)}) collective-permute-start(bf16[160,1536]{1,0:T(8,128)(2,1)} %collective-permute-done.7.refs_1_), channel_id=1, source_target_pairs={{0,1},{1,0},{2,3},{3,2},{4,5},{5,4},{6,7},{7,6},{8,9},{9,8},{10,11... | collective-permute-start | bytes 1474568 | tf_op jit(solution)/shard_map/ppermute | solution.py:332
  85.5 41.8 %collective-permute-start.14 = (bf16[192,1536]{1,0:T(8,128)(2,1)S(1)}, bf16[192,1536]{1,0:T(8,128)(2,1)S(1)}, u32[]{:S(2)}, u32[]{:S(2)}) collective-permute-start(bf16[192,1536]{1,0:T(8,128)(2,1)S(1)} %copy-done.10), channel_id=1, source_target_pairs={{0,2},{2,4},{4,6},{6,0},{1,3},{3,5},{5,7},{7,1},{8,10},{10,12},{12... | collective-permute-start | bytes 1769480 | tf_op jit(solution)/shard_map/ppermute | solution.py:332
  85.6 24.8 %collective-permute-start.13 = (bf16[160,1536]{1,0:T(8,128)(2,1)}, bf16[160,1536]{1,0:T(8,128)(2,1)}, u32[]{:S(2)}, u32[]{:S(2)}) collective-permute-start(bf16[160,1536]{1,0:T(8,128)(2,1)} %copy-done.21), channel_id=1, source_target_pairs={{0,1},{1,0},{2,3},{3,2},{4,5},{5,4},{6,7},{7,6},{8,9},{9,8},{10,11... | collective-permute-start | bytes 1474568 | tf_op jit(solution)/shard_map/ppermute | solution.py:332
  102.7 30.0 %all-to-all-start.1 = ((bf16[8,192,128]{2,1,0:T(8,128)(2,1)}), bf16[8,192,128]{2,1,0:T(8,128)(2,1)S(1)}, u32[]{:S(2)}, u32[]{:S(2)}) async-start(bf16[8,192,128]{2,1,0:T(8,128)(2,1)} %attn.2), calls=%async_computation.1 | async-start | bytes 786432 | tf_op jit(solution)/shard_map/all_to_all | solution.py:409
  107.1 20.3 %collective-permute-start.15 = (bf16[192,1536]{1,0:T(8,128)(2,1)S(1)}, bf16[192,1536]{1,0:T(8,128)(2,1)S(1)}, u32[]{:S(2)}, u32[]{:S(2)}) collective-permute-start(bf16[192,1536]{1,0:T(8,128)(2,1)S(1)} %copy-done.10), channel_id=1, source_target_pairs={{0,6},{2,0},{4,2},{6,4},{1,7},{3,1},{5,3},{7,5},{8,14},{10,8},{12,... | collective-permute-start | bytes 1769480 | tf_op jit(solution)/shard_map/ppermute | solution.py:332
  110.4 29.9 %collective-permute-start.18 = (bf16[192,1536]{1,0:T(8,128)(2,1)S(1)}, bf16[192,1536]{1,0:T(8,128)(2,1)}, u32[]{:S(2)}, u32[]{:S(2)}) collective-permute-start(bf16[192,1536]{1,0:T(8,128)(2,1)S(1)} %copy-done.10), channel_id=1, source_target_pairs={{0,1},{1,0},{2,3},{3,2},{4,5},{5,4},{6,7},{7,6},{8,9},{9,8},{10,11... | collective-permute-start | bytes 1769480 | tf_op jit(solution)/shard_map/ppermute | solution.py:332
  153.1 19.4 %collective-permute-start.23 = (bf16[256,1536]{1,0:T(8,128)(2,1)}, bf16[256,1536]{1,0:T(8,128)(2,1)S(1)}, u32[]{:S(2)}, u32[]{:S(2)}) collective-permute-start(bf16[256,1536]{1,0:T(8,128)(2,1)} %get-tuple-element.25.refs_0_), channel_id=1, source_target_pairs={{0,64},{64,32},{32,96},{96,0},{1,65},{65,33},{33,97},{97,1},{2,66}... | collective-permute-start | bytes 2359304 | tf_op jit(solution)/shard_map/ppermute | solution.py:342
  155.0 19.4 %collective-permute-start.24 = (bf16[256,1536]{1,0:T(8,128)(2,1)}, bf16[256,1536]{1,0:T(8,128)(2,1)}, u32[]{:S(2)}, u32[]{:S(2)}) collective-permute-start(bf16[256,1536]{1,0:T(8,128)(2,1)} %get-tuple-element.25.refs_0_), channel_id=1, source_target_pairs={{0,96},{64,0},{32,64},{96,32},{1,97},{65,1},{33,65},{97,33},{2,98}... | collective-permute-start | bytes 2359304 | tf_op jit(solution)/shard_map/ppermute | solution.py:342
  172.5 25.8 %collective-permute-start.26 = (bf16[128,1536]{1,0:T(8,128)(2,1)S(1)}, bf16[128,1536]{1,0:T(8,128)(2,1)S(1)}, u32[]{:S(2)}, u32[]{:S(2)}) collective-permute-start(bf16[128,1536]{1,0:T(8,128)(2,1)S(1)} %slice.47), channel_id=1, source_target_pairs={{0,64},{64,32},{32,96},{96,0},{1,65},{65,33},{33,97},{97,1},{2,66}... | collective-permute-start | bytes 1179656 | tf_op jit(solution)/shard_map/ppermute | solution.py:342
  175.4 22.8 %collective-permute-start.27 = (bf16[128,1536]{1,0:T(8,128)(2,1)S(1)}, bf16[128,1536]{1,0:T(8,128)(2,1)S(1)}, u32[]{:S(2)}, u32[]{:S(2)}) collective-permute-start(bf16[128,1536]{1,0:T(8,128)(2,1)S(1)} %slice.48), channel_id=1, source_target_pairs={{0,96},{64,0},{32,64},{96,32},{1,97},{65,1},{33,65},{97,33},{2,98}... | collective-permute-start | bytes 1179656 | tf_op jit(solution)/shard_map/ppermute | solution.py:342
  210.1 19.6 %collective-permute-start.25 = (bf16[128,1536]{1,0:T(8,128)(2,1)S(1)}, bf16[128,1536]{1,0:T(8,128)(2,1)S(1)}, u32[]{:S(2)}, u32[]{:S(2)}) collective-permute-start(bf16[128,1536]{1,0:T(8,128)(2,1)S(1)} %copy-done.23), channel_id=1, source_target_pairs={{0,96},{64,0},{32,64},{96,32},{1,97},{65,1},{33,65},{97,33},{2,98}... | collective-permute-start | bytes 1179656 | tf_op jit(solution)/shard_map/ppermute | solution.py:342
  213.2 20.7 %collective-permute-start.30 = (bf16[128,1536]{1,0:T(8,128)(2,1)S(1)}, bf16[128,1536]{1,0:T(8,128)(2,1)S(1)}, u32[]{:S(2)}, u32[]{:S(2)}) collective-permute-start(bf16[128,1536]{1,0:T(8,128)(2,1)S(1)} %copy-done.22), channel_id=1, source_target_pairs={{0,64},{64,32},{32,96},{96,0},{1,65},{65,33},{33,97},{97,1},{2,66}... | collective-permute-start | bytes 1179656 | tf_op jit(solution)/shard_map/ppermute | solution.py:342
  (38 other events, 766.1 us)
Sparse Core Ops, SparseCore 0:
  10.3 77.3 all-gather.2
where the time goes:
time: 255 us; the launch traced here: 252 us
  waiting for transfers between devices  99.3 us (39%)
  Pallas kernels  74.3 us (29%)
  starting transfers between devices  48 us (19%)
  between operations  14.5 us (6%)
  local copies, waits for them, and re-layouts  10.6 us (4%)
  other arithmetic  4.59 us (2%)
    ppermute x24, waiting for transfers between devices, shifted(): lax.ppermute(value, axis, [(i, (i + by) % size) for i in range(size)])  55.9 us
    ppermute x10, waiting for transfers between devices, along_z(): return lax.ppermute(value, ('cfg', 'zhi'), pairs)  38.6 us
    pallas_call x2, Pallas kernels, attention(): pl.pallas_call(functools.partial(attn_kernel, prompt, many), out_shape=ja...  33.9 us
    pallas_call x3, Pallas kernels, mlp(): pl.pallas_call(functools.partial(mlp_kernel, many), out_shape=[jax.ShapeD...  32.1 us
    ppermute x24, starting transfers between devices, shifted(): lax.ppermute(value, axis, [(i, (i + by) % size) for i in range(size)])  20.2 us
    ppermute x10, starting transfers between devices, along_z(): return lax.ppermute(value, ('cfg', 'zhi'), pairs)  11.6 us
    all_to_all x1, starting transfers between devices, local(): got = lax.all_to_all(part, REQ + SEQ, 0, 0, tiled=True)  8.29 us
    all_to_all x2, starting transfers between devices, local(): att = [lax.all_to_all(a, SEQ, 0, 0, tiled=True) for a in att]  7.91 us
  transfers between devices with their start and end apart: 38, of which 17 were waited for; matrix products, arithmetic and copies ran while one was open for 4% of the time, Pallas kernels for 25%

commit v1 on v0

v1 whole, which is shorter than its diff:
```python
import functools
import math

import jax
import jax.numpy as jnp
import numpy as np
from jax import lax
from jax.experimental import pallas as pl
from jax.experimental.pallas import tpu as pltpu
from jax.sharding import Mesh
from jax.sharding import PartitionSpec as P

HEAD = 64
SEQ = ("y", "core")
REQ = ("zhi", "x")
NT = (((1,), (1,)), ((), ()))
NN = (((1,), (0,)), ((), ()))
TN = (((0,), (0,)), ((), ()))
TXT_PAD = 32


def dot(a, b, dims):
    return lax.dot_general(a, b, dims, preferred_element_type=jnp.float32)


def layer_norm(value):
    mean = jnp.mean(value, axis=-1, keepdims=True)
    centered = value - mean
    spread = jnp.mean(centered * centered, axis=-1, keepdims=True)
    return centered * lax.rsqrt(spread + 1e-06)


def attn_kernel(prompt, many, idx_ref, *refs):
    pieces = refs[:many]
    mod_ref, bias_ref, wi_ref, wt_ref, out_ref, x_s, wi_s, wt_s, ai, at, k_s, v_s, q_s, x_sem, w_sem = refs[many:]
    block = x_s.shape[1]
    rows = block - TXT_PAD
    img = many * rows
    keys = many * block
    width = wt_s.shape[0] // 2
    heads = width // HEAD

    def take(s):
        piece = pieces[s] if len(pieces[s].shape) == 2 else pieces[s].at[prompt]
        return pltpu.make_async_copy(piece, x_s.at[s], x_sem.at[s])

    order = [(wi_ref, 0, wi_s, 0), (wi_ref, 2, wi_s, 1), (wi_ref, 1, wi_s, 2), (wt_ref, 2, wt_s, 0), (wt_ref, 1, wt_s, 1)]
    loads = [take(s) for s in range(many)] + [
        pltpu.make_async_copy(src.at[j], dst.at[pl.ds(i * width, width)], w_sem.at[n])
        for n, (src, j, dst, i) in enumerate(order)
    ]
    ahead = 3
    for load in loads[:ahead]:
        load.start()

    def modulated(part, scale, shift):
        normed = layer_norm(part.astype(jnp.float32))
        return (normed * (1.0 + mod_ref[0, scale : scale + 1, :]) + mod_ref[0, shift : shift + 1, :]).astype(
            jnp.bfloat16
        )

    for s in range(many):
        loads[s].wait()
        loads[s + ahead].start()
        ai[s * rows : (s + 1) * rows, :] = modulated(x_s[s, 0:rows, :], 1, 0)
        at[s * TXT_PAD : (s + 1) * TXT_PAD, :] = modulated(x_s[s, rows:block, :], 7, 6)
    for load in loads[many + ahead :]:
        load.start()
    for load in loads[many:]:
        load.wait()
    ones = jnp.ones((16, keys), jnp.bfloat16)
    for h in range(heads):
        v_s[h, HEAD : HEAD + 16, :] = ones
        if h:
            q_s[h, 0 : h * HEAD, :] = jnp.zeros((h * HEAD, img), jnp.bfloat16)
        if h + 1 < heads:
            q_s[h, (h + 1) * HEAD :, :] = jnp.zeros((width - (h + 1) * HEAD, img), jnp.bfloat16)
    wide = 4 * rows

    def some_rows(c, carry):
        span = pl.ds(pl.multiple_of(c * wide, wide), wide)
        a = ai[span, :]
        k_s[span, :] = dot(a, wi_s[2 * width : 3 * width, :], NT).astype(jnp.bfloat16)
        both = dot(wi_s[0 : 2 * width, :], a, NT)
        query = (both[0:width] * (HEAD ** (-0.5) * math.log2(math.e))).astype(jnp.bfloat16)
        for h in range(heads):
            q_s[h, h * HEAD : (h + 1) * HEAD, span] = query[h * HEAD : (h + 1) * HEAD]
            v_s[h, 0:HEAD, span] = both[width + h * HEAD : width + (h + 1) * HEAD].astype(jnp.bfloat16)
        return carry

    lax.fori_loop(0, img // wide, some_rows, 0)
    a_txt = at[...]
    k_s[img:keys, :] = dot(a_txt, wt_s[width : 2 * width, :], NT).astype(jnp.bfloat16)
    v_txt = dot(wt_s[0:width, :], a_txt, NT).astype(jnp.bfloat16)
    for h in range(heads):
        v_s[h, 0:HEAD, img:keys] = v_txt[h * HEAD : (h + 1) * HEAD, :]

    def one_head(h, carry):
        query = q_s[h]
        s_img = dot(k_s[0:img, :], query, NN)
        s_txt = dot(k_s[img:keys, :], query, NN) + bias_ref[0]
        top = jnp.maximum(jnp.max(s_img, axis=0, keepdims=True), jnp.max(s_txt, axis=0, keepdims=True))
        p_img = jnp.exp2(s_img - top).astype(jnp.bfloat16)
        p_txt = jnp.exp2(s_txt - top).astype(jnp.bfloat16)
        o = dot(v_s[h, :, 0:img], p_img, NN) + dot(v_s[h, :, img:keys], p_txt, NN)
        o = (o[0:HEAD] / o[HEAD : HEAD + 1]).astype(jnp.bfloat16)
        for i in range(many):
            out_ref[idx_ref[i], pl.ds(pl.multiple_of(h * HEAD, HEAD), HEAD), :] = o[:, i * rows : (i + 1) * rows]
        return carry

    lax.fori_loop(0, heads, one_head, 0)


def attention(prompt, owners, pieces, mod, bias, w_img, w_txt):
    many = len(pieces)
    block, depth = pieces[0].shape[-2:]
    rows = block - TXT_PAD
    width = w_img.shape[1]
    heads = width // HEAD
    keys = many * block
    once = lambda *zeros: (lambda i, owners: zeros)
    stays = pl.BlockSpec(memory_space=pltpu.HBM)
    bf16 = jnp.bfloat16
    return pl.pallas_call(
        functools.partial(attn_kernel, prompt, many),
        out_shape=jax.ShapeDtypeStruct((many, width, rows), bf16),
        grid_spec=pltpu.PrefetchScalarGridSpec(
            num_scalar_prefetch=1,
            grid=(1,),
            in_specs=[stays] * many
            + [
                pl.BlockSpec((1, 10, depth), once(prompt, 0, 0)),
                pl.BlockSpec((1, many * TXT_PAD, 1), once(prompt, 0, 0)),
                stays,
                stays,
            ],
            out_specs=pl.BlockSpec((many, width, rows), once(0, 0, 0)),
            scratch_shapes=[
                pltpu.VMEM((many, block, depth), bf16),
                pltpu.VMEM((3 * width, depth), bf16),
                pltpu.VMEM((2 * width, depth), bf16),
                pltpu.VMEM((many * rows, depth), bf16),
                pltpu.VMEM((many * TXT_PAD, depth), bf16),
                pltpu.VMEM((keys, width), bf16),
                pltpu.VMEM((heads, HEAD + 16, keys), bf16),
                pltpu.VMEM((heads, width, many * rows), bf16),
                pltpu.SemaphoreType.DMA((many,)),
                pltpu.SemaphoreType.DMA((5,)),
            ],
        ),
        compiler_params=pltpu.CompilerParams(vmem_limit_bytes=56 << 20),
        cost_estimate=pl.CostEstimate(flops=8000000000, bytes_accessed=8000000, transcendentals=0),
        name="attn",
    )(owners, *pieces, mod, bias, w_img, w_txt)


def order_kernel(idx_ref, att_ref, out_ref):
    size = att_ref.shape[1]
    for s in range(att_ref.shape[0]):
        out_ref[s * size : (s + 1) * size, :] = att_ref[idx_ref[s]]


def ordered(owners, att):
    many, size, rows = att.shape
    return pl.pallas_call(
        order_kernel,
        out_shape=jax.ShapeDtypeStruct((many * size, rows), att.dtype),
        grid_spec=pltpu.PrefetchScalarGridSpec(
            num_scalar_prefetch=1,
            grid=(1,),
            in_specs=[pl.BlockSpec(att.shape, lambda i, owners: (0, 0, 0))],
            out_specs=pl.BlockSpec((many * size, rows), lambda i, owners: (0, 0)),
        ),
        cost_estimate=pl.CostEstimate(flops=4000000000, bytes_accessed=8000000, transcendentals=0),
        name="order",
    )(owners, att)


def proj_kernel(many, att_ref, *refs):
    parts = refs[:many]
    img_ref, mod_ref, resid_ref, normed_ref, w_s, sem = refs[many:]
    loads, at = [], 0
    for n, part in enumerate(parts):
        loads.append(pltpu.make_async_copy(part, w_s.at[pl.ds(at, part.shape[0])], sem.at[n]))
        at += part.shape[0]
    for load in loads:
        load.start()
    for load in loads:
        load.wait()
    total = dot(att_ref[...], w_s[...], TN)
    one = (img_ref[0, 0].astype(jnp.float32) + mod_ref[0, 2:3, :] * total).astype(jnp.bfloat16)
    resid_ref[...] = one
    normed = layer_norm(one.astype(jnp.float32)) * (1.0 + mod_ref[0, 4:5, :]) + mod_ref[0, 3:4, :]
    normed_ref[...] = normed.astype(jnp.bfloat16)


def project(prompt, att, parts, img_state, mod):
    rows, depth = img_state.shape[2:]
    many = len(parts)
    once = lambda *zeros: (lambda i: zeros)
    return pl.pallas_call(
        functools.partial(proj_kernel, many),
        out_shape=[jax.ShapeDtypeStruct((rows, depth), jnp.bfloat16)] * 2,
        grid=(1,),
        in_specs=[pl.BlockSpec(att.shape, once(0, 0))]
        + [pl.BlockSpec(memory_space=pltpu.HBM)] * many
        + [
            pl.BlockSpec((1, 1, rows, depth), once(0, prompt, 0, 0)),
            pl.BlockSpec((1, 10, depth), once(prompt, 0, 0)),
        ],
        out_specs=[pl.BlockSpec((rows, depth), once(0, 0))] * 2,
        scratch_shapes=[
            pltpu.VMEM((att.shape[0], depth), jnp.bfloat16),
            pltpu.SemaphoreType.DMA((many,)),
        ],
        compiler_params=pltpu.CompilerParams(vmem_limit_bytes=56 << 20),
        cost_estimate=pl.CostEstimate(flops=8000000000, bytes_accessed=5000000, transcendentals=0),
        name="proj",
    )(att, *parts, img_state, mod)


def mlp_kernel(*refs):
    *pieces, up_ref, down_ref, out_ref, x_s, acc = refs
    step = pl.program_id(0)

    @pl.when(step == 0)
    def _():
        at = 0
        for piece in pieces:
            x_s[at : at + piece.shape[0], :] = piece[...]
            at += piece.shape[0]

    depth = up_ref.shape[-1]
    up = up_ref[...].reshape(-1, depth)
    down = down_ref[...].reshape(-1, depth)
    hidden = jax.nn.gelu(dot(x_s[...], up, NT), approximate=True).astype(jnp.bfloat16)
    term = dot(hidden, down, NN)

    @pl.when(step == 0)
    def _():
        acc[...] = term

    @pl.when(step > 0)
    def _():
        acc[...] += term

    @pl.when(step == pl.num_programs(0) - 1)
    def _():
        out_ref[...] = acc[...].astype(out_ref.dtype)


def mlp(pieces, weights, out_type):
    shards, _, units, width = weights.shape
    many = 16
    count = sum(piece.shape[0] for piece in pieces)
    return pl.pallas_call(
        mlp_kernel,
        out_shape=jax.ShapeDtypeStruct((count, width), out_type),
        grid=(shards // many,),
        in_specs=[
            *[pl.BlockSpec(piece.shape, lambda i: (0, 0)) for piece in pieces],
            pl.BlockSpec((many, 1, units, width), lambda i: (i, 0, 0, 0)),
            pl.BlockSpec((many, 1, units, width), lambda i: (i, 1, 0, 0)),
        ],
        out_specs=pl.BlockSpec((count, width), lambda i: (0, 0)),
        scratch_shapes=[pltpu.VMEM((count, width), jnp.bfloat16), pltpu.VMEM((count, width), jnp.float32)],
        compiler_params=pltpu.CompilerParams(vmem_limit_bytes=56 << 20),
        cost_estimate=pl.CostEstimate(
            flops=4 * count * shards * units * width,
            bytes_accessed=4 * shards * units * width,
            transcendentals=0,
        ),
        name="mlp",
    )(*pieces, weights, weights)


def finish_kernel(mod_ref, w_ref, own_ref, back_ref, *refs):
    *resid, mine_ref, others_ref = refs
    prompts, half, rows = mine_ref.shape
    for p in range(prompts):
        span = slice(p * rows, (p + 1) * rows)
        total = own_ref[span, :] + back_ref[span, :].astype(jnp.float32)
        two = resid[p][...].astype(jnp.float32) + mod_ref[p, 5:6, :] * total
        last = layer_norm(two) * (1.0 + mod_ref[p, 9:10, :]) + mod_ref[p, 8:9, :]
        vel = dot(w_ref[...], last.astype(jnp.bfloat16), (((0,), (1,)), ((), ())))
        mine_ref[p] = vel[0:half]
        others_ref[p] = vel[half:].astype(jnp.bfloat16)


def finish(resid, own, back, mod, w_last):
    prompts = mod.shape[0]
    half = w_last.shape[1] // 2
    shape = (prompts, half, resid[0].shape[0])
    return pl.pallas_call(
        finish_kernel,
        out_shape=[jax.ShapeDtypeStruct(shape, jnp.float32), jax.ShapeDtypeStruct(shape, jnp.bfloat16)],
        compiler_params=pltpu.CompilerParams(vmem_limit_bytes=32 << 20),
        name="finish",
    )(mod, w_last, own, back, *resid)


def shifted(value, axis, by):
    size = lax.axis_size(axis)
    return lax.ppermute(value, axis, [(i, (i + by) % size) for i in range(size)])


def swap(value, axis):
    return shifted(value, axis, 1)


def local(
    img_state,
    txt_state,
    cond_vec,
    text_len,
    latent,
    w_mod,
    w_qkv_img,
    w_qkv_txt,
    w_attn_out,
    w_up,
    w_down,
    w_final,
):
    prompts = img_state.shape[1]
    rows = img_state.shape[2]
    width = img_state.shape[3]
    txt_rows = txt_state.shape[2]
    high = lax.axis_size("y")
    seqs = high * lax.axis_size("core")
    reqs = lax.axis_size("zhi") * lax.axis_size("x")
    everyone = reqs * seqs

    padding = jnp.zeros((prompts, TXT_PAD - txt_rows, width), jnp.bfloat16)
    mine = jnp.concatenate([img_state[0], txt_state[0], padding], axis=1)
    below, above = shifted(mine, "y", 1), shifted(mine, "y", -1)
    far = [shifted(below[p], "y", 1) if p % 2 == 0 else shifted(above[p], "y", -1) for p in range(prompts)]
    pairs = [mine, below, above]
    mates = [swap(block, "core") for block in pairs]
    tokens = [pairs + [far[p]] + mates + [swap(far[p], "core")] for p in range(prompts)]

    weights = lax.all_gather(jnp.stack([w_up, w_down])[None], REQ + SEQ, axis=0, tiled=True)

    cond_act = jax.nn.silu(cond_vec[0]).astype(jnp.bfloat16)
    part = dot(cond_act, w_mod, NT)
    cols = part.shape[1]
    lanes = -(-cols // 128) * 128
    part = jnp.pad(part, ((0, 0), (0, lanes - cols)))
    part = part.reshape(reqs, 1, prompts * lanes // 128, 128)
    part = jnp.broadcast_to(part, (reqs, seqs) + part.shape[2:]).reshape((everyone,) + part.shape[2:])
    got = lax.all_to_all(part, REQ + SEQ, 0, 0, tiled=True)
    got = got.reshape(everyone, prompts, lanes)[:, :, :cols]
    mod = jnp.swapaxes(got, 0, 1).reshape(prompts, 10, width)

    here, core = lax.axis_index("y"), lax.axis_index("core")
    level = (here + jnp.array([0, high - 1, 1, 2], jnp.int32)) % high
    owners = jnp.concatenate([2 * level + core, 2 * level + 1 - core]).astype(jnp.int32)
    inside = jnp.arange(TXT_PAD)
    index = owners[:, None] * txt_rows + inside[None, :]
    live = (inside < txt_rows)[None, None, :] & (index[None] < text_len[0][:, None, None])
    bias = jnp.where(live, 0.0, -1e30).astype(jnp.float32).reshape(prompts, seqs * TXT_PAD, 1)

    att = [
        attention(p, owners, tokens[p], mod, bias, w_qkv_img, w_qkv_txt) for p in range(prompts)
    ]
    late, _ = lax.optimization_barrier((w_attn_out, far[-1]))
    below, above = shifted(late, "y", 1), shifted(late, "y", -1)
    below, above, lead = lax.optimization_barrier((below, above, att[1]))
    cut = late.shape[0] // 2
    far = [shifted(below[:cut], "y", 1), shifted(above[cut:], "y", -1)]
    lead = lax.all_to_all(lead, SEQ, 0, 0, tiled=True)
    lead, far, below, above, last = lax.optimization_barrier((lead, far, below, above, att[0]))
    parts = [late, below, above] + list(far)
    parts = parts + [swap(part, "core") for part in parts]
    last = lax.all_to_all(last, SEQ, 0, 0, tiled=True)
    resid1, normed1 = project(1, ordered(owners, lead), parts, img_state, mod)
    other1 = swap(normed1, "cfg")
    last, other1 = lax.optimization_barrier((ordered(owners, last), other1))
    resid0, normed0 = project(0, last, parts, img_state, mod)
    other0 = swap(normed0, "cfg")
    back = swap(mlp([other0, other1], weights, jnp.bfloat16), "cfg")
    own = mlp([normed0, normed1], weights, jnp.float32)
    resid = [resid0, resid1]

    half = latent.shape[2]
    branch = lax.axis_index("cfg")
    first = branch == 0
    w_last = jnp.where(first, w_final, jnp.concatenate([w_final[:, half:], w_final[:, :half]], axis=1))
    mine, others = finish(resid, own, back, mod, w_last)
    partner = swap(others, "cfg").astype(jnp.float32)
    cond_vel = jnp.where(first, mine, partner)
    uncond_vel = jnp.where(first, partner, mine)
    velocity = uncond_vel + 4.5 * (cond_vel - uncond_vel)
    latent_next = jnp.swapaxes(latent, 1, 2) - 0.04 * velocity
    return jnp.swapaxes(velocity, 1, 2), jnp.swapaxes(latent_next, 1, 2)


def solution(mesh):
    fine = Mesh(np.asarray(mesh.devices).reshape(2, 2, 4, 4, 2), ("cfg", "zhi", "x", "y", "core"))
    every = ("cfg",) + REQ + SEQ
    placed = (
        P("cfg", REQ, SEQ, None),
        P("cfg", REQ, SEQ, None),
        P("cfg", None, None),
        P("cfg", REQ),
        P(REQ, SEQ, "cfg"),
        P(REQ + SEQ, None),
        P(None, SEQ, None),
        P(None, SEQ, None),
        P(SEQ, None),
        P(every, None),
        P(every, None),
        P(),
    )
    return jax.shard_map(
        local,
        mesh=fine,
        in_specs=placed,
        out_specs=(P(REQ, SEQ, "cfg"), P(REQ, SEQ, "cfg")),
        check_vma=False,
    )
```

time: 255 us -> 200 us (0.78)
  waiting for transfers between devices: 99.3 us -> 59.1 us
  starting transfers between devices: 48 us -> 36.5 us
    ppermute x10 -> x0, waiting for transfers between devices: 38.6 us -> none  [along_z(): return lax.ppermute(value, ('cfg', 'zhi'), pairs)]
    ppermute x10 -> x0, starting transfers between devices: 11.6 us -> none  [along_z(): return lax.ppermute(value, ('cfg', 'zhi'), pairs)]
    ppermute x24 -> x22, starting transfers between devices: 20.2 us -> 17.5 us  [shifted(): lax.ppermute(value, axis, [(i, (i + by) % size) for i in range(size)])]
    pallas_call x4 -> x6, Pallas kernels: 39.4 us -> 40.1 us  [the longest x2 23.9 us: mlp(): pl.pallas_call(mlp_kernel, out_shape=jax.ShapeDtypeStruct((count, width),...]
    ppermute x24 -> x22, waiting for transfers between devices: 55.9 us -> 56.5 us  [shifted(): lax.ppermute(value, axis, [(i, (i + by) % size) for i in range(size)])]
  transfers between devices with their start and end apart: 38 -> 26, of which waited for: 17 -> 8; matrix products, arithmetic and copies ran while one was open for 4% -> 4% of each run, Pallas kernels for 25% -> 31%
where the time goes in v1:
time: 200 us; the launch traced here: 199 us
  Pallas kernels  74.2 us (37%)
  waiting for transfers between devices  59.1 us (30%)
  starting transfers between devices  36.5 us (18%)
  between operations  14.5 us (7%)
  local copies, waits for them, and re-layouts  8.39 us (4%)
  other arithmetic  5.72 us (3%)
    ppermute x22, waiting for transfers between devices, shifted(): lax.ppermute(value, axis, [(i, (i + by) % size) for i in range(size)])  56.5 us
    pallas_call x2, Pallas kernels, attention(): pl.pallas_call(functools.partial(attn_kernel, prompt, many), out_shape=ja...  33.2 us
    pallas_call x2, Pallas kernels, mlp(): pl.pallas_call(mlp_kernel, out_shape=jax.ShapeDtypeStruct((count, width),...  23.9 us
    ppermute x22, starting transfers between devices, shifted(): lax.ppermute(value, axis, [(i, (i + by) % size) for i in range(size)])  17.5 us
    pallas_call x2, Pallas kernels, project(): pl.pallas_call(functools.partial(proj_kernel, many), out_shape=[jax.Shape...  11.1 us
    all_to_all x1, starting transfers between devices, local(): got = lax.all_to_all(part, REQ + SEQ, 0, 0, tiled=True)  10.8 us
    pallas_call x2, Pallas kernels, ordered(): pl.pallas_call(order_kernel, out_shape=jax.ShapeDtypeStruct((many * size,...  5 us
    unnamed x43, local copies, waits for them, and re-layouts  4.97 us
  transfers between devices with their start and end apart: 26, of which 8 were waited for; matrix products, arithmetic and copies ran while one was open for 4% of the time, Pallas kernels for 31%

profile of v1, /device:TPU:70, one launch (start us, length us, event | category | flops | bytes accessed | tf_op | source)
XLA Modules:
  0.0 198.7 jit_solution(13601810656651897940)
XLA Ops:
  7.2 1.8 pad_maximum_fusion
  10.7 3.1 %collective-permute-start = (bf16[2,160,1536]{2,1,0:T(8,128)(2,1)S(1)}, bf16[2,160,1536]{2,1,0:T(8,128)(2,1)S(1)}, u32[]{:S(2)}, u32[]{:S(2)}) collective-permute-start(bf16[2,160,1536]{2,1,0:T(8,128)(2,1)S(1)} %maximum_maximum_fusion.refs_0_), channel_id=1, source_target_pairs={{0,6},{2,0},{4,2},{6,4},{1,7},{3,1},{5,3},{7,5},{8,14},{10,8},{12,... | collective-permute-start | bytes 2949128 | tf_op jit(solution)/shard_map/ppermute | solution.py:304
  14.8 10.8 %all-to-all-start = ((f32[64,4,128]{2,1,0:T(4,128)}), f32[64,4,128]{2,1,0:T(4,128)S(1)}, u32[]{:S(2)}, u32[]{:S(2)}) async-start(f32[64,4,128]{2,1,0:T(4,128)} %bitcast.1), calls=%async_computation | async-start | bytes 262144 | tf_op jit(solution)/shard_map/all_to_all | solution.py:351
  26.2 13.0 %collective-permute-done.refs_2_ = bf16[2,160,1536]{2,1,0:T(8,128)(2,1)S(1)} collective-permute-done((bf16[2,160,1536]{2,1,0:T(8,128)(2,1)S(1)}, bf16[2,160,1536]{2,1,0:T(8,128)(2,1)S(1)}, u32[]{:S(2)}, u32[]{:S(2)}) %collective-permute-start) | collective-permute-done | bytes 983072 | tf_op jit(solution)/shard_map/ppermute | solution.py:304
  39.3 3.8 %collective-permute-start.1 = (bf16[160,1536]{1,0:T(8,128)(2,1)S(1)}, bf16[160,1536]{1,0:T(8,128)(2,1)}, u32[]{:S(2)}, u32[]{:S(2)}) collective-permute-start(bf16[160,1536]{1,0:T(8,128)(2,1)S(1)} %slice_bitcast_fusion.1), channel_id=1, source_target_pairs={{0,6},{2,0},{4,2},{6,4},{1,7},{3,1},{5,3},{7,5},{8,14},{10,8},{12,... | collective-permute-start | bytes 1474568 | tf_op jit(solution)/shard_map/ppermute | solution.py:304
  44.9 16.1 %collective-permute-done.1.refs_3_ = bf16[160,1536]{1,0:T(8,128)(2,1)} collective-permute-done((bf16[160,1536]{1,0:T(8,128)(2,1)S(1)}, bf16[160,1536]{1,0:T(8,128)(2,1)}, u32[]{:S(2)}, u32[]{:S(2)}) %collective-permute-start.1) | collective-permute-done | bytes 491552 | tf_op jit(solution)/shard_map/ppermute | solution.py:304
  63.2 7.2 %collective-permute-done.11.refs_3_ = bf16[160,1536]{1,0:T(8,128)(2,1)} collective-permute-done((bf16[160,1536]{1,0:T(8,128)(2,1)S(1)}, bf16[160,1536]{1,0:T(8,128)(2,1)}, u32[]{:S(2)}, u32[]{:S(2)}) %collective-permute-start.11) | collective-permute-done | bytes 491552 | tf_op jit(solution)/shard_map/ppermute | solution.py:304
  70.9 16.5 %attn.2 = bf16[8,192,128]{2,1,0:T(8,128)(2,1)} custom-call(s32[8]{0:T(128)} %get-tuple-element.39.idx_ref, bf16[2,160,1536]{2,1,0:T(8,128)(2,1)} %copy-done.5, bf16[2,160,1536]{2,1,0:T(8,128)(2,1)} %collective-permute-done.4.refs_1_, bf16[2,160,1536]{2,1,0:T(8,128)(2,1)} %copy-done.10, bf16[160,1536]{1,0:T(8,128)(2,1)} %collective-permute-done.1.refs_3_, ...), custom_call_target="tpu_custom_call" | custom-call | flops 8000000000 | bytes 8000000 | tf_op jit(solution)/shard_map/attn/pallas_call | solution.py:124
  88.5 2.1 %collective-permute-start.9 = (bf16[96,1536]{1,0:T(8,128)(2,1)S(1)}, bf16[96,1536]{1,0:T(8,128)(2,1)}, u32[]{:S(2)}, u32[]{:S(2)}) collective-permute-start(bf16[96,1536]{1,0:T(8,128)(2,1)S(1)} %slice.25), channel_id=1, source_target_pairs={{0,2},{2,4},{4,6},{6,0},{1,3},{3,5},{5,7},{7,1},{8,10},{10,12},{12... | collective-permute-start | bytes 884744 | tf_op jit(solution)/shard_map/ppermute | solution.py:304
  90.6 3.7 %all-to-all-start.1 = ((bf16[8,192,128]{2,1,0:T(8,128)(2,1)}), bf16[8,192,128]{2,1,0:T(8,128)(2,1)S(1)}, u32[]{:S(2)}, u32[]{:S(2)}) async-start(bf16[8,192,128]{2,1,0:T(8,128)(2,1)} %attn.2), calls=%async_computation.1 | async-start | bytes 786432 | tf_op jit(solution)/shard_map/all_to_all | solution.py:371
  94.3 16.7 %attn.3 = bf16[8,192,128]{2,1,0:T(8,128)(2,1)} custom-call(s32[8]{0:T(128)} %get-tuple-element.39.idx_ref, bf16[2,160,1536]{2,1,0:T(8,128)(2,1)} %copy-done.5, bf16[2,160,1536]{2,1,0:T(8,128)(2,1)} %collective-permute-done.4.refs_1_, bf16[2,160,1536]{2,1,0:T(8,128)(2,1)} %copy-done.10, bf16[160,1536]{1,0:T(8,128)(2,1)} %collective-permute-done.11.refs_3_, ...), custom_call_target="tpu_custom_call" | custom-call | flops 8000000000 | bytes 8000000 | tf_op jit(solution)/shard_map/attn/pallas_call | solution.py:124
  112.2 4.5 %all-to-all-start.2 = ((bf16[8,192,128]{2,1,0:T(8,128)(2,1)}), bf16[8,192,128]{2,1,0:T(8,128)(2,1)S(1)}, u32[]{:S(2)}, u32[]{:S(2)}) async-start(bf16[8,192,128]{2,1,0:T(8,128)(2,1)} %attn.3), calls=%async_computation.2 | async-start | bytes 786432 | tf_op jit(solution)/shard_map/all_to_all | solution.py:375
  116.7 2.6 %order.3.att_ref = bf16[1536,128]{1,0:T(8,128)(2,1)} custom-call(s32[8]{0:T(128)} %get-tuple-element.39.idx_ref, bf16[8,192,128]{2,1,0:T(8,128)(2,1)} %copy-done.8), custom_call_target="tpu_custom_call" | custom-call | flops 4000000000 | bytes 8000000 | tf_op jit(solution)/shard_map/order/pallas_call | solution.py:165
  120.1 5.5 %proj.2 = (bf16[128,1536]{1,0:T(8,128)(2,1)}, bf16[128,1536]{1,0:T(8,128)(2,1)}) custom-call(bf16[1536,128]{1,0:T(8,128)(2,1)} %order.3.att_ref, bf16[192,1536]{1,0:T(8,128)(2,1)} %refs_0_.1, bf16[192,1536]{1,0:T(8,128)(2,1)} %copy-done.12, bf16[192,1536]{1,0:T(8,128)(2,1)} %copy-done.14, bf16[96,1536]{1,0:T(8,128)(2,1)} %collective-permute-done.9.refs_3_, ...), custom_call_target="tpu_custom_call" | custom-call | flops 8000000000 | bytes 5000000 | tf_op jit(solution)/shard_map/proj/pallas_call | solution.py:201
  127.2 2.6 %all-to-all-done.2.att_ref = bf16[8,192,128]{2,1,0:T(8,128)(2,1)S(1)} async-done(((bf16[8,192,128]{2,1,0:T(8,128)(2,1)}), bf16[8,192,128]{2,1,0:T(8,128)(2,1)S(1)}, u32[]{:S(2)}, u32[]{:S(2)}) %all-to-all-start.2) | async-done | bytes 393248 | tf_op jit(solution)/shard_map/all_to_all | solution.py:375
  130.5 2.4 %order.2.att_ref = bf16[1536,128]{1,0:T(8,128)(2,1)} custom-call(s32[8]{0:T(128)} %get-tuple-element.39.idx_ref, bf16[8,192,128]{2,1,0:T(8,128)(2,1)} %copy-done.9), custom_call_target="tpu_custom_call" | custom-call | flops 4000000000 | bytes 8000000 | tf_op jit(solution)/shard_map/order/pallas_call | solution.py:165
  133.0 4.4 %collective-permute-done.18.refs_1_ = bf16[128,1536]{1,0:T(8,128)(2,1)S(1)} collective-permute-done((bf16[128,1536]{1,0:T(8,128)(2,1)}, bf16[128,1536]{1,0:T(8,128)(2,1)S(1)}, u32[]{:S(2)}, u32[]{:S(2)}) %collective-permute-start.18) | collective-permute-done | bytes 393248 | tf_op jit(solution)/shard_map/ppermute | solution.py:304
  137.4 5.6 %proj.3 = (bf16[128,1536]{1,0:T(8,128)(2,1)}, bf16[128,1536]{1,0:T(8,128)(2,1)}) custom-call(bf16[1536,128]{1,0:T(8,128)(2,1)} %order.2.att_ref, bf16[192,1536]{1,0:T(8,128)(2,1)} %refs_0_.1, bf16[192,1536]{1,0:T(8,128)(2,1)} %copy-done.12, bf16[192,1536]{1,0:T(8,128)(2,1)} %copy-done.14, bf16[96,1536]{1,0:T(8,128)(2,1)} %collective-permute-done.9.refs_3_, ...), custom_call_target="tpu_custom_call" | custom-call | flops 8000000000 | bytes 5000000 | tf_op jit(solution)/shard_map/proj/pallas_call | solution.py:201
  144.7 9.3 %collective-permute-done.19.refs_0_ = bf16[128,1536]{1,0:T(8,128)(2,1)S(1)} collective-permute-done((bf16[128,1536]{1,0:T(8,128)(2,1)}, bf16[128,1536]{1,0:T(8,128)(2,1)S(1)}, u32[]{:S(2)}, u32[]{:S(2)}) %collective-permute-start.19) | collective-permute-done | bytes 393248 | tf_op jit(solution)/shard_map/ppermute | solution.py:304
  154.7 11.8 %mlp.3 = bf16[256,1536]{1,0:T(8,128)(2,1)} custom-call(bf16[128,1536]{1,0:T(8,128)(2,1)} %copy-done.7, bf16[128,1536]{1,0:T(8,128)(2,1)} %copy-done.6, bf16[64,2,48,1536]{3,2,1,0:T(8,128)(2,1)} %bitcast.36, bf16[64,2,48,1536]{3,2,1,0:T(8,128)(2,1)} %bitcast.37), custom_call_target="tpu_custom_call" | custom-call | flops 4831838208 | bytes 18874368 | tf_op jit(solution)/shard_map/mlp/pallas_call | solution.py:256
  168.5 12.2 %mlp.2.own_ref = f32[256,1536]{1,0:T(8,128)} custom-call(bf16[128,1536]{1,0:T(8,128)(2,1)} %get-tuple-element.32.refs_0_, bf16[128,1536]{1,0:T(8,128)(2,1)} %get-tuple-element.30.refs_1_, bf16[64,2,48,1536]{3,2,1,0:T(8,128)(2,1)} %bitcast.38, bf16[64,2,48,1536]{3,2,1,0:T(8,128)(2,1)} %bitcast.39), custom_call_target="tpu_custom_call" | custom-call | flops 4831838208 | bytes 18874368 | tf_op jit(solution)/shard_map/mlp/pallas_call | solution.py:256
  180.6 4.4 %collective-permute-done.20.back_ref = bf16[256,1536]{1,0:T(8,128)(2,1)S(1)} collective-permute-done((bf16[256,1536]{1,0:T(8,128)(2,1)}, bf16[256,1536]{1,0:T(8,128)(2,1)S(1)}, u32[]{:S(2)}, u32[]{:S(2)}) %collective-permute-start.20) | collective-permute-done | bytes 786464 | tf_op jit(solution)/shard_map/ppermute | solution.py:304
  187.4 1.8 collective-permute-start.21
  189.2 2.0 %collective-permute-done.21 = bf16[2,32,128]{2,1,0:T(8,128)(2,1)S(1)} collective-permute-done((bf16[2,32,128]{2,1,0:T(8,128)(2,1)S(1)}, bf16[2,32,128]{2,1,0:T(8,128)(2,1)S(1)}, u32[]{:S(2)}, u32[]{:S(2)}) %collective-permute-start.21) | collective-permute-done | bytes 16416 | tf_op jit(solution)/shard_map/ppermute | solution.py:304
  (112 shorter events, 20.4 us)
Async XLA Ops:
  7.2 146.8 %all-gather.3.cloned.1.call-start = ((), (), s32[]{:S(2)}) async-start(), calls=%async_computation.3 | async-start | bytes 19169280 | tf_op jit(solution)/shard_map/all_gather | solution.py:342
  10.7 28.6 %collective-permute-start = (bf16[2,160,1536]{2,1,0:T(8,128)(2,1)S(1)}, bf16[2,160,1536]{2,1,0:T(8,128)(2,1)S(1)}, u32[]{:S(2)}, u32[]{:S(2)}) collective-permute-start(bf16[2,160,1536]{2,1,0:T(8,128)(2,1)S(1)} %maximum_maximum_fusion.refs_0_), channel_id=1, source_target_pairs={{0,6},{2,0},{4,2},{6,4},{1,7},{3,1},{5,3},{7,5},{8,14},{10,8},{12,... | collective-permute-start | bytes 2949128 | tf_op jit(solution)/shard_map/ppermute | solution.py:304
  13.8 29.5 %collective-permute-start.4 = (bf16[2,160,1536]{2,1,0:T(8,128)(2,1)S(1)}, bf16[2,160,1536]{2,1,0:T(8,128)(2,1)}, u32[]{:S(2)}, u32[]{:S(2)}) collective-permute-start(bf16[2,160,1536]{2,1,0:T(8,128)(2,1)S(1)} %maximum_maximum_fusion.refs_0_), channel_id=1, source_target_pairs={{0,2},{2,4},{4,6},{6,0},{1,3},{3,5},{5,7},{7,1},{8,10},{10,12},{12... | collective-permute-start | bytes 2949128 | tf_op jit(solution)/shard_map/ppermute | solution.py:304
  13.8 49.4 %collective-permute-start.5 = (bf16[2,160,1536]{2,1,0:T(8,128)(2,1)S(1)}, bf16[2,160,1536]{2,1,0:T(8,128)(2,1)}, u32[]{:S(2)}, u32[]{:S(2)}) collective-permute-start(bf16[2,160,1536]{2,1,0:T(8,128)(2,1)S(1)} %maximum_maximum_fusion.refs_0_), channel_id=1, source_target_pairs={{0,1},{1,0},{2,3},{3,2},{4,5},{5,4},{6,7},{7,6},{8,9},{9,8},{10,11... | collective-permute-start | bytes 2949128 | tf_op jit(solution)/shard_map/ppermute | solution.py:304
  14.8 47.4 %all-to-all-start = ((f32[64,4,128]{2,1,0:T(4,128)}), f32[64,4,128]{2,1,0:T(4,128)S(1)}, u32[]{:S(2)}, u32[]{:S(2)}) async-start(f32[64,4,128]{2,1,0:T(4,128)} %bitcast.1), calls=%async_computation | async-start | bytes 262144 | tf_op jit(solution)/shard_map/all_to_all | solution.py:351
  39.3 21.7 %collective-permute-start.1 = (bf16[160,1536]{1,0:T(8,128)(2,1)S(1)}, bf16[160,1536]{1,0:T(8,128)(2,1)}, u32[]{:S(2)}, u32[]{:S(2)}) collective-permute-start(bf16[160,1536]{1,0:T(8,128)(2,1)S(1)} %slice_bitcast_fusion.1), channel_id=1, source_target_pairs={{0,6},{2,0},{4,2},{6,4},{1,7},{3,1},{5,3},{7,5},{8,14},{10,8},{12,... | collective-permute-start | bytes 1474568 | tf_op jit(solution)/shard_map/ppermute | solution.py:304
  43.2 27.8 %collective-permute-start.7 = (bf16[2,160,1536]{2,1,0:T(8,128)(2,1)S(1)}, bf16[2,160,1536]{2,1,0:T(8,128)(2,1)}, u32[]{:S(2)}, u32[]{:S(2)}) collective-permute-start(bf16[2,160,1536]{2,1,0:T(8,128)(2,1)S(1)} %collective-permute-done.refs_2_), channel_id=1, source_target_pairs={{0,1},{1,0},{2,3},{3,2},{4,5},{5,4},{6,7},{7,6},{8,9},{9,8},{10,11... | collective-permute-start | bytes 2949128 | tf_op jit(solution)/shard_map/ppermute | solution.py:304
  43.3 27.2 %collective-permute-start.6 = (bf16[2,160,1536]{2,1,0:T(8,128)(2,1)}, bf16[2,160,1536]{2,1,0:T(8,128)(2,1)}, u32[]{:S(2)}, u32[]{:S(2)}) collective-permute-start(bf16[2,160,1536]{2,1,0:T(8,128)(2,1)} %collective-permute-done.4.refs_1_), channel_id=1, source_target_pairs={{0,1},{1,0},{2,3},{3,2},{4,5},{5,4},{6,7},{7,6},{8,9},{9,8},{10,11... | collective-permute-start | bytes 2949128 | tf_op jit(solution)/shard_map/ppermute | solution.py:304
  44.8 25.6 %collective-permute-start.11 = (bf16[160,1536]{1,0:T(8,128)(2,1)S(1)}, bf16[160,1536]{1,0:T(8,128)(2,1)}, u32[]{:S(2)}, u32[]{:S(2)}) collective-permute-start(bf16[160,1536]{1,0:T(8,128)(2,1)S(1)} %slice_bitcast_fusion), channel_id=1, source_target_pairs={{0,2},{2,4},{4,6},{6,0},{1,3},{3,5},{5,7},{7,1},{8,10},{10,12},{12... | collective-permute-start | bytes 1474568 | tf_op jit(solution)/shard_map/ppermute | solution.py:304
  61.1 9.4 %collective-permute-start.8 = (bf16[160,1536]{1,0:T(8,128)(2,1)}, bf16[160,1536]{1,0:T(8,128)(2,1)}, u32[]{:S(2)}, u32[]{:S(2)}) collective-permute-start(bf16[160,1536]{1,0:T(8,128)(2,1)} %collective-permute-done.1.refs_3_), channel_id=1, source_target_pairs={{0,1},{1,0},{2,3},{3,2},{4,5},{5,4},{6,7},{7,6},{8,9},{9,8},{10,11... | collective-permute-start | bytes 1474568 | tf_op jit(solution)/shard_map/ppermute | solution.py:304
  63.2 24.3 %collective-permute-start.2 = (bf16[192,1536]{1,0:T(8,128)(2,1)}, bf16[192,1536]{1,0:T(8,128)(2,1)S(1)}, u32[]{:S(2)}, u32[]{:S(2)}) collective-permute-start(bf16[192,1536]{1,0:T(8,128)(2,1)} %refs_0_.1), channel_id=1, source_target_pairs={{0,2},{2,4},{4,6},{6,0},{1,3},{3,5},{5,7},{7,1},{8,10},{10,12},{12... | collective-permute-start | bytes 1769480 | tf_op jit(solution)/shard_map/ppermute | solution.py:304
  70.4 17.1 %collective-permute-start.3 = (bf16[192,1536]{1,0:T(8,128)(2,1)}, bf16[192,1536]{1,0:T(8,128)(2,1)S(1)}, u32[]{:S(2)}, u32[]{:S(2)}) collective-permute-start(bf16[192,1536]{1,0:T(8,128)(2,1)} %refs_0_.1), channel_id=1, source_target_pairs={{0,6},{2,0},{4,2},{6,4},{1,7},{3,1},{5,3},{7,5},{8,14},{10,8},{12,... | collective-permute-start | bytes 1769480 | tf_op jit(solution)/shard_map/ppermute | solution.py:304
  70.4 48.8 %collective-permute-start.13 = (bf16[192,1536]{1,0:T(8,128)(2,1)}, bf16[192,1536]{1,0:T(8,128)(2,1)}, u32[]{:S(2)}, u32[]{:S(2)}) collective-permute-start(bf16[192,1536]{1,0:T(8,128)(2,1)} %refs_0_.1), channel_id=1, source_target_pairs={{0,1},{1,0},{2,3},{3,2},{4,5},{5,4},{6,7},{7,6},{8,9},{9,8},{10,11... | collective-permute-start | bytes 1769480 | tf_op jit(solution)/shard_map/ppermute | solution.py:304
  70.5 23.9 %collective-permute-start.12 = (bf16[160,1536]{1,0:T(8,128)(2,1)}, bf16[160,1536]{1,0:T(8,128)(2,1)}, u32[]{:S(2)}, u32[]{:S(2)}) collective-permute-start(bf16[160,1536]{1,0:T(8,128)(2,1)} %collective-permute-done.11.refs_3_), channel_id=1, source_target_pairs={{0,1},{1,0},{2,3},{3,2},{4,5},{5,4},{6,7},{7,6},{8,9},{9,8},{10,11... | collective-permute-start | bytes 1474568 | tf_op jit(solution)/shard_map/ppermute | solution.py:304
  88.4 22.7 %collective-permute-start.10 = (bf16[96,1536]{1,0:T(8,128)(2,1)S(1)}, bf16[96,1536]{1,0:T(8,128)(2,1)}, u32[]{:S(2)}, u32[]{:S(2)}) collective-permute-start(bf16[96,1536]{1,0:T(8,128)(2,1)S(1)} %slice.26), channel_id=1, source_target_pairs={{0,6},{2,0},{4,2},{6,4},{1,7},{3,1},{5,3},{7,5},{8,14},{10,8},{12,... | collective-permute-start | bytes 884744 | tf_op jit(solution)/shard_map/ppermute | solution.py:304
  88.5 22.5 %collective-permute-start.9 = (bf16[96,1536]{1,0:T(8,128)(2,1)S(1)}, bf16[96,1536]{1,0:T(8,128)(2,1)}, u32[]{:S(2)}, u32[]{:S(2)}) collective-permute-start(bf16[96,1536]{1,0:T(8,128)(2,1)S(1)} %slice.25), channel_id=1, source_target_pairs={{0,2},{2,4},{4,6},{6,0},{1,3},{3,5},{5,7},{7,1},{8,10},{10,12},{12... | collective-permute-start | bytes 884744 | tf_op jit(solution)/shard_map/ppermute | solution.py:304
  90.6 20.4 %all-to-all-start.1 = ((bf16[8,192,128]{2,1,0:T(8,128)(2,1)}), bf16[8,192,128]{2,1,0:T(8,128)(2,1)S(1)}, u32[]{:S(2)}, u32[]{:S(2)}) async-start(bf16[8,192,128]{2,1,0:T(8,128)(2,1)} %attn.2), calls=%async_computation.1 | async-start | bytes 786432 | tf_op jit(solution)/shard_map/all_to_all | solution.py:371
  111.1 8.2 %collective-permute-start.14 = (bf16[192,1536]{1,0:T(8,128)(2,1)S(1)}, bf16[192,1536]{1,0:T(8,128)(2,1)S(1)}, u32[]{:S(2)}, u32[]{:S(2)}) collective-permute-start(bf16[192,1536]{1,0:T(8,128)(2,1)S(1)} %copy-done.13), channel_id=1, source_target_pairs={{0,1},{1,0},{2,3},{3,2},{4,5},{5,4},{6,7},{7,6},{8,9},{9,8},{10,11... | collective-permute-start | bytes 1769480 | tf_op jit(solution)/shard_map/ppermute | solution.py:304
  111.5 7.7 %collective-permute-start.15 = (bf16[192,1536]{1,0:T(8,128)(2,1)S(1)}, bf16[192,1536]{1,0:T(8,128)(2,1)}, u32[]{:S(2)}, u32[]{:S(2)}) collective-permute-start(bf16[192,1536]{1,0:T(8,128)(2,1)S(1)} %copy-done.15), channel_id=1, source_target_pairs={{0,1},{1,0},{2,3},{3,2},{4,5},{5,4},{6,7},{7,6},{8,9},{9,8},{10,11... | collective-permute-start | bytes 1769480 | tf_op jit(solution)/shard_map/ppermute | solution.py:304
  111.7 7.6 %collective-permute-start.16 = (bf16[96,1536]{1,0:T(8,128)(2,1)}, bf16[96,1536]{1,0:T(8,128)(2,1)}, u32[]{:S(2)}, u32[]{:S(2)}) collective-permute-start(bf16[96,1536]{1,0:T(8,128)(2,1)} %collective-permute-done.9.refs_3_), channel_id=1, source_target_pairs={{0,1},{1,0},{2,3},{3,2},{4,5},{5,4},{6,7},{7,6},{8,9},{9,8},{10,11... | collective-permute-start | bytes 884744 | tf_op jit(solution)/shard_map/ppermute | solution.py:304
  112.2 17.6 %all-to-all-start.2 = ((bf16[8,192,128]{2,1,0:T(8,128)(2,1)}), bf16[8,192,128]{2,1,0:T(8,128)(2,1)S(1)}, u32[]{:S(2)}, u32[]{:S(2)}) async-start(bf16[8,192,128]{2,1,0:T(8,128)(2,1)} %attn.3), calls=%async_computation.2 | async-start | bytes 786432 | tf_op jit(solution)/shard_map/all_to_all | solution.py:375
  125.6 11.8 %collective-permute-start.18 = (bf16[128,1536]{1,0:T(8,128)(2,1)}, bf16[128,1536]{1,0:T(8,128)(2,1)S(1)}, u32[]{:S(2)}, u32[]{:S(2)}) collective-permute-start(bf16[128,1536]{1,0:T(8,128)(2,1)} %get-tuple-element.30.refs_1_), channel_id=1, source_target_pairs={{0,64},{64,0},{1,65},{65,1},{2,66},{66,2},{3,67},{67,3},{4,68},{68... | collective-permute-start | bytes 1179656 | tf_op jit(solution)/shard_map/ppermute | solution.py:304
  143.0 11.0 %collective-permute-start.19 = (bf16[128,1536]{1,0:T(8,128)(2,1)}, bf16[128,1536]{1,0:T(8,128)(2,1)S(1)}, u32[]{:S(2)}, u32[]{:S(2)}) collective-permute-start(bf16[128,1536]{1,0:T(8,128)(2,1)} %get-tuple-element.32.refs_0_), channel_id=1, source_target_pairs={{0,64},{64,0},{1,65},{65,1},{2,66},{66,2},{3,67},{67,3},{4,68},{68... | collective-permute-start | bytes 1179656 | tf_op jit(solution)/shard_map/ppermute | solution.py:304
  166.5 18.5 %collective-permute-start.20 = (bf16[256,1536]{1,0:T(8,128)(2,1)}, bf16[256,1536]{1,0:T(8,128)(2,1)S(1)}, u32[]{:S(2)}, u32[]{:S(2)}) collective-permute-start(bf16[256,1536]{1,0:T(8,128)(2,1)} %mlp.3), channel_id=1, source_target_pairs={{0,64},{64,0},{1,65},{65,1},{2,66},{66,2},{3,67},{67,3},{4,68},{68... | collective-permute-start | bytes 2359304 | tf_op jit(solution)/shard_map/ppermute | solution.py:304
  (23 other events, 307.8 us)
Sparse Core Ops, SparseCore 0:
  11.1 125.8 all-gather.2

commit v2 on v1

--- a/solution.py
+++ b/solution.py
@@ -154,69 +154,68 @@
     )(owners, *pieces, mod, bias, w_img, w_txt)
 
 
-def order_kernel(idx_ref, att_ref, out_ref):
+def pass_on(value):
+    anywhere = pl.BlockSpec(memory_space=pl.ANY)
+    return pl.pallas_call(
+        lambda value_ref, out_ref: None,
+        out_shape=jax.ShapeDtypeStruct(value.shape, value.dtype),
+        in_specs=[anywhere],
+        out_specs=anywhere,
+        input_output_aliases={0: 0},
+        cost_estimate=pl.CostEstimate(flops=4000000000, bytes_accessed=8000000, transcendentals=0),
+        name="pass_on",
+    )(value)
+
+
+def proj_kernel(many, idx_ref, att_ref, *refs):
+    parts = refs[:many]
+    img_ref, mod_ref, resid_ref, normed_ref, w_s, att_s, sem = refs[many:]
     size = att_ref.shape[1]
-    for s in range(att_ref.shape[0]):
-        out_ref[s * size : (s + 1) * size, :] = att_ref[idx_ref[s]]
-
-
-def ordered(owners, att):
-    many, size, rows = att.shape
-    return pl.pallas_call(
-        order_kernel,
-        out_shape=jax.ShapeDtypeStruct((many * size, rows), att.dtype),
-        grid_spec=pltpu.PrefetchScalarGridSpec(
-            num_scalar_prefetch=1,
-            grid=(1,),
-            in_specs=[pl.BlockSpec(att.shape, lambda i, owners: (0, 0, 0))],
-            out_specs=pl.BlockSpec((many * size, rows), lambda i, owners: (0, 0)),
-        ),
-        cost_estimate=pl.CostEstimate(flops=4000000000, bytes_accessed=8000000, transcendentals=0),
-        name="order",
-    )(owners, att)
-
-
-def proj_kernel(many, att_ref, *refs):
-    parts = refs[:many]
-    img_ref, mod_ref, resid_ref, normed_ref, w_s, sem = refs[many:]
     loads, at = [], 0
     for n, part in enumerate(parts):
         loads.append(pltpu.make_async_copy(part, w_s.at[pl.ds(at, part.shape[0])], sem.at[n]))
         at += part.shape[0]
     for load in loads:
         load.start()
+    for s in range(att_ref.shape[0]):
+        att_s[s * size : (s + 1) * size, :] = att_ref[idx_ref[s]]
     for load in loads:
         load.wait()
-    total = dot(att_ref[...], w_s[...], TN)
+    total = dot(att_s[...], w_s[...], TN)
     one = (img_ref[0, 0].astype(jnp.float32) + mod_ref[0, 2:3, :] * total).astype(jnp.bfloat16)
     resid_ref[...] = one
     normed = layer_norm(one.astype(jnp.float32)) * (1.0 + mod_ref[0, 4:5, :]) + mod_ref[0, 3:4, :]
     normed_ref[...] = normed.astype(jnp.bfloat16)
 
 
-def project(prompt, att, parts, img_state, mod):
+def project(prompt, owners, att, parts, img_state, mod):
     rows, depth = img_state.shape[2:]
     many = len(parts)
-    once = lambda *zeros: (lambda i: zeros)
+    total = att.shape[0] * att.shape[1]
+    once = lambda *zeros: (lambda i, owners: zeros)
     return pl.pallas_call(
         functools.partial(proj_kernel, many),
         out_shape=[jax.ShapeDtypeStruct((rows, depth), jnp.bfloat16)] * 2,
-        grid=(1,),
-        in_specs=[pl.BlockSpec(att.shape, once(0, 0))]
-        + [pl.BlockSpec(memory_space=pltpu.HBM)] * many
-        + [
-            pl.BlockSpec((1, 1, rows, depth), once(0, prompt, 0, 0)),
-            pl.BlockSpec((1, 10, depth), once(prompt, 0, 0)),
-        ],
-        out_specs=[pl.BlockSpec((rows, depth), once(0, 0))] * 2,
-        scratch_shapes=[
-            pltpu.VMEM((att.shape[0], depth), jnp.bfloat16),
-            pltpu.SemaphoreType.DMA((many,)),
-        ],
+        grid_spec=pltpu.PrefetchScalarGridSpec(
+            num_scalar_prefetch=1,
+            grid=(1,),
+            in_specs=[pl.BlockSpec(att.shape, once(0, 0, 0))]
+            + [pl.BlockSpec(memory_space=pltpu.HBM)] * many
+            + [
+                pl.BlockSpec((1, 1, rows, depth), once(0, prompt, 0, 0)),
+                pl.BlockSpec((1, 10, depth), once(prompt, 0, 0)),
+            ],
+            out_specs=[pl.BlockSpec((rows, depth), once(0, 0))] * 2,
+            scratch_shapes=[
+                pltpu.VMEM((total, depth), jnp.bfloat16),
+                pltpu.VMEM((total, rows), jnp.bfloat16),
+                pltpu.SemaphoreType.DMA((many,)),
+            ],
+        ),
         compiler_params=pltpu.CompilerParams(vmem_limit_bytes=56 << 20),
         cost_estimate=pl.CostEstimate(flops=8000000000, bytes_accessed=5000000, transcendentals=0),
         name="proj",
-    )(att, *parts, img_state, mod)
+    )(owners, att, *parts, img_state, mod)
 
 
 def mlp_kernel(*refs):
@@ -251,7 +250,7 @@
 
 def mlp(pieces, weights, out_type):
     shards, _, units, width = weights.shape
-    many = 16
+    many = 32
     count = sum(piece.shape[0] for piece in pieces)
     return pl.pallas_call(
         mlp_kernel,
@@ -373,12 +372,11 @@
     parts = [late, below, above] + list(far)
     parts = parts + [swap(part, "core") for part in parts]
     last = lax.all_to_all(last, SEQ, 0, 0, tiled=True)
-    resid1, normed1 = project(1, ordered(owners, lead), parts, img_state, mod)
+    resid1, normed1 = project(1, owners, lead, parts, img_state, mod)
     other1 = swap(normed1, "cfg")
-    last, other1 = lax.optimization_barrier((ordered(owners, last), other1))
-    resid0, normed0 = project(0, last, parts, img_state, mod)
+    resid0, normed0 = project(0, owners, pass_on(last), parts, img_state, mod)
     other0 = swap(normed0, "cfg")
-    back = swap(mlp([other0, other1], weights, jnp.bfloat16), "cfg")
+    back = swap(mlp([other0, pass_on(other1)], weights, jnp.bfloat16), "cfg")
     own = mlp([normed0, normed1], weights, jnp.float32)
     resid = [resid0, resid1]
 

time: 200 us -> 200 us (level)
  waiting for transfers between devices: 59.1 us -> 68 us
  Pallas kernels: 74.2 us -> 67.8 us
  starting transfers between devices: 36.5 us -> 33.6 us
    all_to_all x1, waiting for transfers between devices: 2.57 us -> 11.2 us  [local(): last = lax.all_to_all(last, SEQ, 0, 0, tiled=True)]
    pallas_call x2, Pallas kernels: 5 us -> 0.01 us  [pass_on(): pl.pallas_call(lambda value_ref, out_ref: None, out_shape=jax.ShapeDtypeS...]
    ppermute x22, starting transfers between devices: 17.5 us -> 14.6 us  [shifted(): lax.ppermute(value, axis, [(i, (i + by) % size) for i in range(size)])]
    pallas_call x2, Pallas kernels: 23.9 us -> 21.4 us  [mlp(): pl.pallas_call(mlp_kernel, out_shape=jax.ShapeDtypeStruct((count, width),...]
  transfers between devices with their start and end apart: 26 -> 26, of which waited for: 8 -> 8; matrix products, arithmetic and copies ran while one was open for 4% -> 4% of each run, Pallas kernels for 31% -> 28%
where the time goes in v2:
time: 200 us; the launch traced here: 199 us
  waiting for transfers between devices  68 us (34%)
  Pallas kernels  67.8 us (34%)
  starting transfers between devices  33.6 us (17%)
  between operations  14.5 us (7%)
  local copies, waits for them, and re-layouts  9.08 us (5%)
  other arithmetic  5.69 us (3%)
    ppermute x22, waiting for transfers between devices, shifted(): lax.ppermute(value, axis, [(i, (i + by) % size) for i in range(size)])  56.8 us
    pallas_call x2, Pallas kernels, attention(): pl.pallas_call(functools.partial(attn_kernel, prompt, many), out_shape=ja...  33.2 us
    pallas_call x2, Pallas kernels, mlp(): pl.pallas_call(mlp_kernel, out_shape=jax.ShapeDtypeStruct((count, width),...  21.4 us
    ppermute x22, starting transfers between devices, shifted(): lax.ppermute(value, axis, [(i, (i + by) % size) for i in range(size)])  14.6 us
    pallas_call x2, Pallas kernels, project(): pl.pallas_call(functools.partial(proj_kernel, many), out_shape=[jax.Shape...  12.2 us
    all_to_all x1, waiting for transfers between devices, local(): last = lax.all_to_all(last, SEQ, 0, 0, tiled=True)  11.2 us
    all_to_all x1, starting transfers between devices, local(): got = lax.all_to_all(part, REQ + SEQ, 0, 0, tiled=True)  10.8 us
    unnamed x43, local copies, waits for them, and re-layouts  5.67 us
  transfers between devices with their start and end apart: 26, of which 8 were waited for; matrix products, arithmetic and copies ran while one was open for 4% of the time, Pallas kernels for 28%

profile of v2, /device:TPU:70, one launch (start us, length us, event | category | flops | bytes accessed | tf_op | source)
XLA Modules:
  0.0 199.0 jit_solution(7310789899682758182)
XLA Ops:
  7.2 1.8 pad_maximum_fusion
  9.1 1.5 maximum_maximum_fusion.refs_0_
  10.7 3.1 %collective-permute-start = (bf16[2,160,1536]{2,1,0:T(8,128)(2,1)S(1)}, bf16[2,160,1536]{2,1,0:T(8,128)(2,1)S(1)}, u32[]{:S(2)}, u32[]{:S(2)}) collective-permute-start(bf16[2,160,1536]{2,1,0:T(8,128)(2,1)S(1)} %maximum_maximum_fusion.refs_0_), channel_id=1, source_target_pairs={{0,6},{2,0},{4,2},{6,4},{1,7},{3,1},{5,3},{7,5},{8,14},{10,8},{12,... | collective-permute-start | bytes 2949128 | tf_op jit(solution)/shard_map/ppermute | solution.py:303
  14.8 10.8 %all-to-all-start = ((f32[64,4,128]{2,1,0:T(4,128)}), f32[64,4,128]{2,1,0:T(4,128)S(1)}, u32[]{:S(2)}, u32[]{:S(2)}) async-start(f32[64,4,128]{2,1,0:T(4,128)} %bitcast.1), calls=%async_computation | async-start | bytes 262144 | tf_op jit(solution)/shard_map/all_to_all | solution.py:350
  26.2 13.0 %collective-permute-done.refs_2_ = bf16[2,160,1536]{2,1,0:T(8,128)(2,1)S(1)} collective-permute-done((bf16[2,160,1536]{2,1,0:T(8,128)(2,1)S(1)}, bf16[2,160,1536]{2,1,0:T(8,128)(2,1)S(1)}, u32[]{:S(2)}, u32[]{:S(2)}) %collective-permute-start) | collective-permute-done | bytes 983072 | tf_op jit(solution)/shard_map/ppermute | solution.py:303
  39.3 3.8 %collective-permute-start.1 = (bf16[160,1536]{1,0:T(8,128)(2,1)S(1)}, bf16[160,1536]{1,0:T(8,128)(2,1)}, u32[]{:S(2)}, u32[]{:S(2)}) collective-permute-start(bf16[160,1536]{1,0:T(8,128)(2,1)S(1)} %slice_bitcast_fusion.1), channel_id=1, source_target_pairs={{0,6},{2,0},{4,2},{6,4},{1,7},{3,1},{5,3},{7,5},{8,14},{10,8},{12,... | collective-permute-start | bytes 1474568 | tf_op jit(solution)/shard_map/ppermute | solution.py:303
  44.9 16.1 %collective-permute-done.1.refs_3_ = bf16[160,1536]{1,0:T(8,128)(2,1)} collective-permute-done((bf16[160,1536]{1,0:T(8,128)(2,1)S(1)}, bf16[160,1536]{1,0:T(8,128)(2,1)}, u32[]{:S(2)}, u32[]{:S(2)}) %collective-permute-start.1) | collective-permute-done | bytes 491552 | tf_op jit(solution)/shard_map/ppermute | solution.py:303
  63.1 7.3 %collective-permute-done.11.refs_3_ = bf16[160,1536]{1,0:T(8,128)(2,1)} collective-permute-done((bf16[160,1536]{1,0:T(8,128)(2,1)S(1)}, bf16[160,1536]{1,0:T(8,128)(2,1)}, u32[]{:S(2)}, u32[]{:S(2)}) %collective-permute-start.11) | collective-permute-done | bytes 491552 | tf_op jit(solution)/shard_map/ppermute | solution.py:303
  70.5 16.5 %attn.2 = bf16[8,192,128]{2,1,0:T(8,128)(2,1)} custom-call(s32[8]{0:T(128)} %get-tuple-element.35.idx_ref, bf16[2,160,1536]{2,1,0:T(8,128)(2,1)} %copy-done.5, bf16[2,160,1536]{2,1,0:T(8,128)(2,1)} %collective-permute-done.4.refs_1_, bf16[2,160,1536]{2,1,0:T(8,128)(2,1)} %copy-done.10, bf16[160,1536]{1,0:T(8,128)(2,1)} %collective-permute-done.1.refs_3_, ...), custom_call_target="tpu_custom_call" | custom-call | flops 8000000000 | bytes 8000000 | tf_op jit(solution)/shard_map/attn/pallas_call | solution.py:124
  88.1 2.1 %collective-permute-start.9 = (bf16[96,1536]{1,0:T(8,128)(2,1)S(1)}, bf16[96,1536]{1,0:T(8,128)(2,1)}, u32[]{:S(2)}, u32[]{:S(2)}) collective-permute-start(bf16[96,1536]{1,0:T(8,128)(2,1)S(1)} %slice.25), channel_id=1, source_target_pairs={{0,2},{2,4},{4,6},{6,0},{1,3},{3,5},{5,7},{7,1},{8,10},{10,12},{12... | collective-permute-start | bytes 884744 | tf_op jit(solution)/shard_map/ppermute | solution.py:303
  90.2 3.7 %all-to-all-start.1 = ((bf16[8,192,128]{2,1,0:T(8,128)(2,1)}), bf16[8,192,128]{2,1,0:T(8,128)(2,1)S(1)}, u32[]{:S(2)}, u32[]{:S(2)}) async-start(bf16[8,192,128]{2,1,0:T(8,128)(2,1)} %attn.2), calls=%async_computation.1 | async-start | bytes 786432 | tf_op jit(solution)/shard_map/all_to_all | solution.py:370
  93.9 16.7 %attn.3 = bf16[8,192,128]{2,1,0:T(8,128)(2,1)} custom-call(s32[8]{0:T(128)} %get-tuple-element.35.idx_ref, bf16[2,160,1536]{2,1,0:T(8,128)(2,1)} %copy-done.5, bf16[2,160,1536]{2,1,0:T(8,128)(2,1)} %collective-permute-done.4.refs_1_, bf16[2,160,1536]{2,1,0:T(8,128)(2,1)} %copy-done.10, bf16[160,1536]{1,0:T(8,128)(2,1)} %collective-permute-done.11.refs_3_, ...), custom_call_target="tpu_custom_call" | custom-call | flops 8000000000 | bytes 8000000 | tf_op jit(solution)/shard_map/attn/pallas_call | solution.py:124
  111.4 4.5 %all-to-all-start.2 = ((bf16[8,192,128]{2,1,0:T(8,128)(2,1)}), bf16[8,192,128]{2,1,0:T(8,128)(2,1)S(1)}, u32[]{:S(2)}, u32[]{:S(2)}) async-start(bf16[8,192,128]{2,1,0:T(8,128)(2,1)} %attn.3), calls=%async_computation.2 | async-start | bytes 786432 | tf_op jit(solution)/shard_map/all_to_all | solution.py:374
  117.7 11.2 %all-to-all-done.2.value_ref = bf16[8,192,128]{2,1,0:T(8,128)(2,1)S(1)} async-done(((bf16[8,192,128]{2,1,0:T(8,128)(2,1)}), bf16[8,192,128]{2,1,0:T(8,128)(2,1)S(1)}, u32[]{:S(2)}, u32[]{:S(2)}) %all-to-all-start.2) | async-done | bytes 393248 | tf_op jit(solution)/shard_map/all_to_all | solution.py:374
  129.7 6.1 %proj.3 = (bf16[128,1536]{1,0:T(8,128)(2,1)}, bf16[128,1536]{1,0:T(8,128)(2,1)}) custom-call(s32[8]{0:T(128)} %get-tuple-element.35.idx_ref, bf16[8,192,128]{2,1,0:T(8,128)(2,1)} %copy-done.8, bf16[192,1536]{1,0:T(8,128)(2,1)} %refs_0_.1, bf16[192,1536]{1,0:T(8,128)(2,1)} %copy-done.12, bf16[192,1536]{1,0:T(8,128)(2,1)} %copy-done.14, ...), custom_call_target="tpu_custom_call" | custom-call | flops 8000000000 | bytes 5000000 | tf_op jit(solution)/shard_map/proj/pallas_call | solution.py:196
  135.8 1.6 collective-permute-start.19
  137.5 6.1 %proj.2 = (bf16[128,1536]{1,0:T(8,128)(2,1)}, bf16[128,1536]{1,0:T(8,128)(2,1)}) custom-call(s32[8]{0:T(128)} %get-tuple-element.35.idx_ref, bf16[8,192,128]{2,1,0:T(8,128)(2,1)} %pass_on.2.att_ref, bf16[192,1536]{1,0:T(8,128)(2,1)} %refs_0_.1, bf16[192,1536]{1,0:T(8,128)(2,1)} %copy-done.12, bf16[192,1536]{1,0:T(8,128)(2,1)} %copy-done.14, ...), custom_call_target="tpu_custom_call" | custom-call | flops 8000000000 | bytes 5000000 | tf_op jit(solution)/shard_map/proj/pallas_call | solution.py:196
  144.5 3.6 %collective-permute-done.19.value_ref = bf16[128,1536]{1,0:T(8,128)(2,1)S(1)} collective-permute-done((bf16[128,1536]{1,0:T(8,128)(2,1)}, bf16[128,1536]{1,0:T(8,128)(2,1)S(1)}, u32[]{:S(2)}, u32[]{:S(2)}) %collective-permute-start.19) | collective-permute-done | bytes 393248 | tf_op jit(solution)/shard_map/ppermute | solution.py:303
  148.9 6.5 %collective-permute-done.18.refs_0_ = bf16[128,1536]{1,0:T(8,128)(2,1)S(1)} collective-permute-done((bf16[128,1536]{1,0:T(8,128)(2,1)}, bf16[128,1536]{1,0:T(8,128)(2,1)S(1)}, u32[]{:S(2)}, u32[]{:S(2)}) %collective-permute-start.18) | collective-permute-done | bytes 393248 | tf_op jit(solution)/shard_map/ppermute | solution.py:303
  156.2 10.5 %mlp.3 = bf16[256,1536]{1,0:T(8,128)(2,1)} custom-call(bf16[128,1536]{1,0:T(8,128)(2,1)} %copy-done.7, bf16[128,1536]{1,0:T(8,128)(2,1)} %pass_on.3.refs_1_, bf16[64,2,48,1536]{3,2,1,0:T(8,128)(2,1)} %bitcast.36, bf16[64,2,48,1536]{3,2,1,0:T(8,128)(2,1)} %bitcast.37), custom_call_target="tpu_custom_call" | custom-call | flops 4831838208 | bytes 18874368 | tf_op jit(solution)/shard_map/mlp/pallas_call | solution.py:255
  167.3 10.9 %mlp.2.own_ref = f32[256,1536]{1,0:T(8,128)} custom-call(bf16[128,1536]{1,0:T(8,128)(2,1)} %get-tuple-element.27.refs_0_, bf16[128,1536]{1,0:T(8,128)(2,1)} %get-tuple-element.29.refs_1_, bf16[64,2,48,1536]{3,2,1,0:T(8,128)(2,1)} %bitcast.38, bf16[64,2,48,1536]{3,2,1,0:T(8,128)(2,1)} %bitcast.39), custom_call_target="tpu_custom_call" | custom-call | flops 4831838208 | bytes 18874368 | tf_op jit(solution)/shard_map/mlp/pallas_call | solution.py:255
  178.2 7.1 %collective-permute-done.20.back_ref = bf16[256,1536]{1,0:T(8,128)(2,1)S(1)} collective-permute-done((bf16[256,1536]{1,0:T(8,128)(2,1)}, bf16[256,1536]{1,0:T(8,128)(2,1)S(1)}, u32[]{:S(2)}, u32[]{:S(2)}) %collective-permute-start.20) | collective-permute-done | bytes 786464 | tf_op jit(solution)/shard_map/ppermute | solution.py:303
  185.3 1.4 copy-done.1
  188.3 3.1 %collective-permute-done.21 = bf16[2,32,128]{2,1,0:T(8,128)(2,1)S(1)} collective-permute-done((bf16[2,32,128]{2,1,0:T(8,128)(2,1)S(1)}, bf16[2,32,128]{2,1,0:T(8,128)(2,1)S(1)}, u32[]{:S(2)}, u32[]{:S(2)}) %collective-permute-start.21) | collective-permute-done | bytes 16416 | tf_op jit(solution)/shard_map/ppermute | solution.py:303
  (112 shorter events, 15.5 us)
Async XLA Ops:
  7.2 148.2 %all-gather.3.cloned.1.call-start = ((), (), s32[]{:S(2)}) async-start(), calls=%async_computation.3 | async-start | bytes 19169280 | tf_op jit(solution)/shard_map/all_gather | solution.py:341
  10.7 28.6 %collective-permute-start = (bf16[2,160,1536]{2,1,0:T(8,128)(2,1)S(1)}, bf16[2,160,1536]{2,1,0:T(8,128)(2,1)S(1)}, u32[]{:S(2)}, u32[]{:S(2)}) collective-permute-start(bf16[2,160,1536]{2,1,0:T(8,128)(2,1)S(1)} %maximum_maximum_fusion.refs_0_), channel_id=1, source_target_pairs={{0,6},{2,0},{4,2},{6,4},{1,7},{3,1},{5,3},{7,5},{8,14},{10,8},{12,... | collective-permute-start | bytes 2949128 | tf_op jit(solution)/shard_map/ppermute | solution.py:303
  13.8 29.5 %collective-permute-start.4 = (bf16[2,160,1536]{2,1,0:T(8,128)(2,1)S(1)}, bf16[2,160,1536]{2,1,0:T(8,128)(2,1)}, u32[]{:S(2)}, u32[]{:S(2)}) collective-permute-start(bf16[2,160,1536]{2,1,0:T(8,128)(2,1)S(1)} %maximum_maximum_fusion.refs_0_), channel_id=1, source_target_pairs={{0,2},{2,4},{4,6},{6,0},{1,3},{3,5},{5,7},{7,1},{8,10},{10,12},{12... | collective-permute-start | bytes 2949128 | tf_op jit(solution)/shard_map/ppermute | solution.py:303
  13.8 49.4 %collective-permute-start.5 = (bf16[2,160,1536]{2,1,0:T(8,128)(2,1)S(1)}, bf16[2,160,1536]{2,1,0:T(8,128)(2,1)}, u32[]{:S(2)}, u32[]{:S(2)}) collective-permute-start(bf16[2,160,1536]{2,1,0:T(8,128)(2,1)S(1)} %maximum_maximum_fusion.refs_0_), channel_id=1, source_target_pairs={{0,1},{1,0},{2,3},{3,2},{4,5},{5,4},{6,7},{7,6},{8,9},{9,8},{10,11... | collective-permute-start | bytes 2949128 | tf_op jit(solution)/shard_map/ppermute | solution.py:303
  14.8 47.3 %all-to-all-start = ((f32[64,4,128]{2,1,0:T(4,128)}), f32[64,4,128]{2,1,0:T(4,128)S(1)}, u32[]{:S(2)}, u32[]{:S(2)}) async-start(f32[64,4,128]{2,1,0:T(4,128)} %bitcast.1), calls=%async_computation | async-start | bytes 262144 | tf_op jit(solution)/shard_map/all_to_all | solution.py:350
  39.3 21.7 %collective-permute-start.1 = (bf16[160,1536]{1,0:T(8,128)(2,1)S(1)}, bf16[160,1536]{1,0:T(8,128)(2,1)}, u32[]{:S(2)}, u32[]{:S(2)}) collective-permute-start(bf16[160,1536]{1,0:T(8,128)(2,1)S(1)} %slice_bitcast_fusion.1), channel_id=1, source_target_pairs={{0,6},{2,0},{4,2},{6,4},{1,7},{3,1},{5,3},{7,5},{8,14},{10,8},{12,... | collective-permute-start | bytes 1474568 | tf_op jit(solution)/shard_map/ppermute | solution.py:303
  43.2 27.3 %collective-permute-start.7 = (bf16[2,160,1536]{2,1,0:T(8,128)(2,1)S(1)}, bf16[2,160,1536]{2,1,0:T(8,128)(2,1)}, u32[]{:S(2)}, u32[]{:S(2)}) collective-permute-start(bf16[2,160,1536]{2,1,0:T(8,128)(2,1)S(1)} %collective-permute-done.refs_2_), channel_id=1, source_target_pairs={{0,1},{1,0},{2,3},{3,2},{4,5},{5,4},{6,7},{7,6},{8,9},{9,8},{10,11... | collective-permute-start | bytes 2949128 | tf_op jit(solution)/shard_map/ppermute | solution.py:303
  43.3 27.2 %collective-permute-start.6 = (bf16[2,160,1536]{2,1,0:T(8,128)(2,1)}, bf16[2,160,1536]{2,1,0:T(8,128)(2,1)}, u32[]{:S(2)}, u32[]{:S(2)}) collective-permute-start(bf16[2,160,1536]{2,1,0:T(8,128)(2,1)} %collective-permute-done.4.refs_1_), channel_id=1, source_target_pairs={{0,1},{1,0},{2,3},{3,2},{4,5},{5,4},{6,7},{7,6},{8,9},{9,8},{10,11... | collective-permute-start | bytes 2949128 | tf_op jit(solution)/shard_map/ppermute | solution.py:303
  44.8 25.6 %collective-permute-start.11 = (bf16[160,1536]{1,0:T(8,128)(2,1)S(1)}, bf16[160,1536]{1,0:T(8,128)(2,1)}, u32[]{:S(2)}, u32[]{:S(2)}) collective-permute-start(bf16[160,1536]{1,0:T(8,128)(2,1)S(1)} %slice_bitcast_fusion), channel_id=1, source_target_pairs={{0,2},{2,4},{4,6},{6,0},{1,3},{3,5},{5,7},{7,1},{8,10},{10,12},{12... | collective-permute-start | bytes 1474568 | tf_op jit(solution)/shard_map/ppermute | solution.py:303
  63.1 23.9 %collective-permute-start.2 = (bf16[192,1536]{1,0:T(8,128)(2,1)}, bf16[192,1536]{1,0:T(8,128)(2,1)S(1)}, u32[]{:S(2)}, u32[]{:S(2)}) collective-permute-start(bf16[192,1536]{1,0:T(8,128)(2,1)} %refs_0_.1), channel_id=1, source_target_pairs={{0,2},{2,4},{4,6},{6,0},{1,3},{3,5},{5,7},{7,1},{8,10},{10,12},{12... | collective-permute-start | bytes 1769480 | tf_op jit(solution)/shard_map/ppermute | solution.py:303
  70.4 16.6 %collective-permute-start.3 = (bf16[192,1536]{1,0:T(8,128)(2,1)}, bf16[192,1536]{1,0:T(8,128)(2,1)S(1)}, u32[]{:S(2)}, u32[]{:S(2)}) collective-permute-start(bf16[192,1536]{1,0:T(8,128)(2,1)} %refs_0_.1), channel_id=1, source_target_pairs={{0,6},{2,0},{4,2},{6,4},{1,7},{3,1},{5,3},{7,5},{8,14},{10,8},{12,... | collective-permute-start | bytes 1769480 | tf_op jit(solution)/shard_map/ppermute | solution.py:303
  70.4 23.5 %collective-permute-start.12 = (bf16[160,1536]{1,0:T(8,128)(2,1)}, bf16[160,1536]{1,0:T(8,128)(2,1)}, u32[]{:S(2)}, u32[]{:S(2)}) collective-permute-start(bf16[160,1536]{1,0:T(8,128)(2,1)} %collective-permute-done.11.refs_3_), channel_id=1, source_target_pairs={{0,1},{1,0},{2,3},{3,2},{4,5},{5,4},{6,7},{7,6},{8,9},{9,8},{10,11... | collective-permute-start | bytes 1474568 | tf_op jit(solution)/shard_map/ppermute | solution.py:303
  87.9 22.7 %collective-permute-start.10 = (bf16[96,1536]{1,0:T(8,128)(2,1)S(1)}, bf16[96,1536]{1,0:T(8,128)(2,1)S(1)}, u32[]{:S(2)}, u32[]{:S(2)}) collective-permute-start(bf16[96,1536]{1,0:T(8,128)(2,1)S(1)} %slice.26), channel_id=1, source_target_pairs={{0,6},{2,0},{4,2},{6,4},{1,7},{3,1},{5,3},{7,5},{8,14},{10,8},{12,... | collective-permute-start | bytes 884744 | tf_op jit(solution)/shard_map/ppermute | solution.py:303
  88.1 22.5 %collective-permute-start.9 = (bf16[96,1536]{1,0:T(8,128)(2,1)S(1)}, bf16[96,1536]{1,0:T(8,128)(2,1)}, u32[]{:S(2)}, u32[]{:S(2)}) collective-permute-start(bf16[96,1536]{1,0:T(8,128)(2,1)S(1)} %slice.25), channel_id=1, source_target_pairs={{0,2},{2,4},{4,6},{6,0},{1,3},{3,5},{5,7},{7,1},{8,10},{10,12},{12... | collective-permute-start | bytes 884744 | tf_op jit(solution)/shard_map/ppermute | solution.py:303
  90.2 20.5 %all-to-all-start.1 = ((bf16[8,192,128]{2,1,0:T(8,128)(2,1)}), bf16[8,192,128]{2,1,0:T(8,128)(2,1)S(1)}, u32[]{:S(2)}, u32[]{:S(2)}) async-start(bf16[8,192,128]{2,1,0:T(8,128)(2,1)} %attn.2), calls=%async_computation.1 | async-start | bytes 786432 | tf_op jit(solution)/shard_map/all_to_all | solution.py:370
  111.4 17.5 %all-to-all-start.2 = ((bf16[8,192,128]{2,1,0:T(8,128)(2,1)}), bf16[8,192,128]{2,1,0:T(8,128)(2,1)S(1)}, u32[]{:S(2)}, u32[]{:S(2)}) async-start(bf16[8,192,128]{2,1,0:T(8,128)(2,1)} %attn.3), calls=%async_computation.2 | async-start | bytes 786432 | tf_op jit(solution)/shard_map/all_to_all | solution.py:374
  115.8 13.8 %collective-permute-start.13 = (bf16[192,1536]{1,0:T(8,128)(2,1)}, bf16[192,1536]{1,0:T(8,128)(2,1)}, u32[]{:S(2)}, u32[]{:S(2)}) collective-permute-start(bf16[192,1536]{1,0:T(8,128)(2,1)} %refs_0_.1), channel_id=1, source_target_pairs={{0,1},{1,0},{2,3},{3,2},{4,5},{5,4},{6,7},{7,6},{8,9},{9,8},{10,11... | collective-permute-start | bytes 1769480 | tf_op jit(solution)/shard_map/ppermute | solution.py:303
  116.3 13.3 %collective-permute-start.14 = (bf16[192,1536]{1,0:T(8,128)(2,1)S(1)}, bf16[192,1536]{1,0:T(8,128)(2,1)}, u32[]{:S(2)}, u32[]{:S(2)}) collective-permute-start(bf16[192,1536]{1,0:T(8,128)(2,1)S(1)} %copy-done.13), channel_id=1, source_target_pairs={{0,1},{1,0},{2,3},{3,2},{4,5},{5,4},{6,7},{7,6},{8,9},{9,8},{10,11... | collective-permute-start | bytes 1769480 | tf_op jit(solution)/shard_map/ppermute | solution.py:303
  116.4 13.3 %collective-permute-start.15 = (bf16[192,1536]{1,0:T(8,128)(2,1)S(1)}, bf16[192,1536]{1,0:T(8,128)(2,1)}, u32[]{:S(2)}, u32[]{:S(2)}) collective-permute-start(bf16[192,1536]{1,0:T(8,128)(2,1)S(1)} %copy-done.15), channel_id=1, source_target_pairs={{0,1},{1,0},{2,3},{3,2},{4,5},{5,4},{6,7},{7,6},{8,9},{9,8},{10,11... | collective-permute-start | bytes 1769480 | tf_op jit(solution)/shard_map/ppermute | solution.py:303
  117.1 12.6 %collective-permute-start.16 = (bf16[96,1536]{1,0:T(8,128)(2,1)}, bf16[96,1536]{1,0:T(8,128)(2,1)}, u32[]{:S(2)}, u32[]{:S(2)}) collective-permute-start(bf16[96,1536]{1,0:T(8,128)(2,1)} %collective-permute-done.9.refs_3_), channel_id=1, source_target_pairs={{0,1},{1,0},{2,3},{3,2},{4,5},{5,4},{6,7},{7,6},{8,9},{9,8},{10,11... | collective-permute-start | bytes 884744 | tf_op jit(solution)/shard_map/ppermute | solution.py:303
  117.2 12.4 %collective-permute-start.17 = (bf16[96,1536]{1,0:T(8,128)(2,1)}, bf16[96,1536]{1,0:T(8,128)(2,1)}, u32[]{:S(2)}, u32[]{:S(2)}) collective-permute-start(bf16[96,1536]{1,0:T(8,128)(2,1)} %copy-done.20), channel_id=1, source_target_pairs={{0,1},{1,0},{2,3},{3,2},{4,5},{5,4},{6,7},{7,6},{8,9},{9,8},{10,11... | collective-permute-start | bytes 884744 | tf_op jit(solution)/shard_map/ppermute | solution.py:303
  135.8 12.3 %collective-permute-start.19 = (bf16[128,1536]{1,0:T(8,128)(2,1)}, bf16[128,1536]{1,0:T(8,128)(2,1)S(1)}, u32[]{:S(2)}, u32[]{:S(2)}) collective-permute-start(bf16[128,1536]{1,0:T(8,128)(2,1)} %get-tuple-element.29.refs_1_), channel_id=1, source_target_pairs={{0,64},{64,0},{1,65},{65,1},{2,66},{66,2},{3,67},{67,3},{4,68},{68... | collective-permute-start | bytes 1179656 | tf_op jit(solution)/shard_map/ppermute | solution.py:303
  143.5 11.9 %collective-permute-start.18 = (bf16[128,1536]{1,0:T(8,128)(2,1)}, bf16[128,1536]{1,0:T(8,128)(2,1)S(1)}, u32[]{:S(2)}, u32[]{:S(2)}) collective-permute-start(bf16[128,1536]{1,0:T(8,128)(2,1)} %get-tuple-element.27.refs_0_), channel_id=1, source_target_pairs={{0,64},{64,0},{1,65},{65,1},{2,66},{66,2},{3,67},{67,3},{4,68},{68... | collective-permute-start | bytes 1179656 | tf_op jit(solution)/shard_map/ppermute | solution.py:303
  166.7 18.6 %collective-permute-start.20 = (bf16[256,1536]{1,0:T(8,128)(2,1)}, bf16[256,1536]{1,0:T(8,128)(2,1)S(1)}, u32[]{:S(2)}, u32[]{:S(2)}) collective-permute-start(bf16[256,1536]{1,0:T(8,128)(2,1)} %mlp.3), channel_id=1, source_target_pairs={{0,64},{64,0},{1,65},{65,1},{2,66},{66,2},{3,67},{67,3},{4,68},{68... | collective-permute-start | bytes 2359304 | tf_op jit(solution)/shard_map/ppermute | solution.py:303
  (23 other events, 349.7 us)
Sparse Core Ops, SparseCore 0:
  11.1 125.6 all-gather.2

commit v3 on v2

--- a/solution.py
+++ b/solution.py
@@ -59,11 +59,19 @@
             jnp.bfloat16
         )
 
-    for s in range(many):
-        loads[s].wait()
-        loads[s + ahead].start()
-        ai[s * rows : (s + 1) * rows, :] = modulated(x_s[s, 0:rows, :], 1, 0)
-        at[s * TXT_PAD : (s + 1) * TXT_PAD, :] = modulated(x_s[s, rows:block, :], 7, 6)
+    def one_piece(s, carry):
+        for n in range(many):
+
+            @pl.when(s == n)
+            def _(n=n):
+                loads[n].wait()
+                loads[n + ahead].start()
+
+        ai[pl.ds(pl.multiple_of(s * rows, rows), rows), :] = modulated(x_s[s, 0:rows, :], 1, 0)
+        at[pl.ds(pl.multiple_of(s * TXT_PAD, TXT_PAD), TXT_PAD), :] = modulated(x_s[s, rows:block, :], 7, 6)
+        return carry
+
+    lax.fori_loop(0, many, one_piece, 0)
     for load in loads[many + ahead :]:
         load.start()
     for load in loads[many:]:

time: 200 us -> 200 us (level)
  no operation moved by 1% of the time
where the time goes in v3:
time: 200 us; the launch traced here: 199 us
  waiting for transfers between devices  68.3 us (34%)
  Pallas kernels  67.8 us (34%)
  starting transfers between devices  33.4 us (17%)
  between operations  14.5 us (7%)
  local copies, waits for them, and re-layouts  9.08 us (5%)
  other arithmetic  5.69 us (3%)
    ppermute x22, waiting for transfers between devices, shifted(): lax.ppermute(value, axis, [(i, (i + by) % size) for i in range(size)])  57.1 us
    pallas_call x2, Pallas kernels, attention(): pl.pallas_call(functools.partial(attn_kernel, prompt, many), out_shape=ja...  33.2 us
    pallas_call x2, Pallas kernels, mlp(): pl.pallas_call(mlp_kernel, out_shape=jax.ShapeDtypeStruct((count, width),...  21.4 us
    ppermute x22, starting transfers between devices, shifted(): lax.ppermute(value, axis, [(i, (i + by) % size) for i in range(size)])  14.4 us
    pallas_call x2, Pallas kernels, project(): pl.pallas_call(functools.partial(proj_kernel, many), out_shape=[jax.Shape...  12.2 us
    all_to_all x1, waiting for transfers between devices, local(): last = lax.all_to_all(last, SEQ, 0, 0, tiled=True)  11.2 us
    all_to_all x1, starting transfers between devices, local(): got = lax.all_to_all(part, REQ + SEQ, 0, 0, tiled=True)  10.8 us
    unnamed x43, local copies, waits for them, and re-layouts  5.67 us
  transfers between devices with their start and end apart: 26, of which 8 were waited for; matrix products, arithmetic and copies ran while one was open for 4% of the time, Pallas kernels for 28%

profile of v3, /device:TPU:70, one launch (start us, length us, event | category | flops | bytes accessed | tf_op | source)
XLA Modules:
  0.0 199.1 jit_solution(534944779566021876)
XLA Ops:
  7.2 1.8 pad_maximum_fusion
  9.1 1.5 maximum_maximum_fusion.refs_0_
  10.7 3.1 %collective-permute-start = (bf16[2,160,1536]{2,1,0:T(8,128)(2,1)S(1)}, bf16[2,160,1536]{2,1,0:T(8,128)(2,1)S(1)}, u32[]{:S(2)}, u32[]{:S(2)}) collective-permute-start(bf16[2,160,1536]{2,1,0:T(8,128)(2,1)S(1)} %maximum_maximum_fusion.refs_0_), channel_id=1, source_target_pairs={{0,6},{2,0},{4,2},{6,4},{1,7},{3,1},{5,3},{7,5},{8,14},{10,8},{12,... | collective-permute-start | bytes 2949128 | tf_op jit(solution)/shard_map/ppermute | solution.py:311
  14.8 10.8 %all-to-all-start = ((f32[64,4,128]{2,1,0:T(4,128)}), f32[64,4,128]{2,1,0:T(4,128)S(1)}, u32[]{:S(2)}, u32[]{:S(2)}) async-start(f32[64,4,128]{2,1,0:T(4,128)} %bitcast.1), calls=%async_computation | async-start | bytes 262144 | tf_op jit(solution)/shard_map/all_to_all | solution.py:358
  26.2 13.0 %collective-permute-done.refs_2_ = bf16[2,160,1536]{2,1,0:T(8,128)(2,1)S(1)} collective-permute-done((bf16[2,160,1536]{2,1,0:T(8,128)(2,1)S(1)}, bf16[2,160,1536]{2,1,0:T(8,128)(2,1)S(1)}, u32[]{:S(2)}, u32[]{:S(2)}) %collective-permute-start) | collective-permute-done | bytes 983072 | tf_op jit(solution)/shard_map/ppermute | solution.py:311
  39.3 3.8 %collective-permute-start.1 = (bf16[160,1536]{1,0:T(8,128)(2,1)S(1)}, bf16[160,1536]{1,0:T(8,128)(2,1)}, u32[]{:S(2)}, u32[]{:S(2)}) collective-permute-start(bf16[160,1536]{1,0:T(8,128)(2,1)S(1)} %slice_bitcast_fusion.1), channel_id=1, source_target_pairs={{0,6},{2,0},{4,2},{6,4},{1,7},{3,1},{5,3},{7,5},{8,14},{10,8},{12,... | collective-permute-start | bytes 1474568 | tf_op jit(solution)/shard_map/ppermute | solution.py:311
  44.9 16.1 %collective-permute-done.1.refs_3_ = bf16[160,1536]{1,0:T(8,128)(2,1)} collective-permute-done((bf16[160,1536]{1,0:T(8,128)(2,1)S(1)}, bf16[160,1536]{1,0:T(8,128)(2,1)}, u32[]{:S(2)}, u32[]{:S(2)}) %collective-permute-start.1) | collective-permute-done | bytes 491552 | tf_op jit(solution)/shard_map/ppermute | solution.py:311
  63.1 7.3 %collective-permute-done.11.refs_3_ = bf16[160,1536]{1,0:T(8,128)(2,1)} collective-permute-done((bf16[160,1536]{1,0:T(8,128)(2,1)S(1)}, bf16[160,1536]{1,0:T(8,128)(2,1)}, u32[]{:S(2)}, u32[]{:S(2)}) %collective-permute-start.11) | collective-permute-done | bytes 491552 | tf_op jit(solution)/shard_map/ppermute | solution.py:311
  70.5 16.5 %attn.2 = bf16[8,192,128]{2,1,0:T(8,128)(2,1)} custom-call(s32[8]{0:T(128)} %get-tuple-element.35.idx_ref, bf16[2,160,1536]{2,1,0:T(8,128)(2,1)} %copy-done.5, bf16[2,160,1536]{2,1,0:T(8,128)(2,1)} %collective-permute-done.4.refs_1_, bf16[2,160,1536]{2,1,0:T(8,128)(2,1)} %copy-done.10, bf16[160,1536]{1,0:T(8,128)(2,1)} %collective-permute-done.1.refs_3_, ...), custom_call_target="tpu_custom_call" | custom-call | flops 8000000000 | bytes 8000000 | tf_op jit(solution)/shard_map/attn/pallas_call | solution.py:132
  88.1 2.1 %collective-permute-start.9 = (bf16[96,1536]{1,0:T(8,128)(2,1)S(1)}, bf16[96,1536]{1,0:T(8,128)(2,1)}, u32[]{:S(2)}, u32[]{:S(2)}) collective-permute-start(bf16[96,1536]{1,0:T(8,128)(2,1)S(1)} %slice.25), channel_id=1, source_target_pairs={{0,2},{2,4},{4,6},{6,0},{1,3},{3,5},{5,7},{7,1},{8,10},{10,12},{12... | collective-permute-start | bytes 884744 | tf_op jit(solution)/shard_map/ppermute | solution.py:311
  90.2 3.6 %all-to-all-start.1 = ((bf16[8,192,128]{2,1,0:T(8,128)(2,1)}), bf16[8,192,128]{2,1,0:T(8,128)(2,1)S(1)}, u32[]{:S(2)}, u32[]{:S(2)}) async-start(bf16[8,192,128]{2,1,0:T(8,128)(2,1)} %attn.2), calls=%async_computation.1 | async-start | bytes 786432 | tf_op jit(solution)/shard_map/all_to_all | solution.py:378
  93.9 16.7 %attn.3 = bf16[8,192,128]{2,1,0:T(8,128)(2,1)} custom-call(s32[8]{0:T(128)} %get-tuple-element.35.idx_ref, bf16[2,160,1536]{2,1,0:T(8,128)(2,1)} %copy-done.5, bf16[2,160,1536]{2,1,0:T(8,128)(2,1)} %collective-permute-done.4.refs_1_, bf16[2,160,1536]{2,1,0:T(8,128)(2,1)} %copy-done.10, bf16[160,1536]{1,0:T(8,128)(2,1)} %collective-permute-done.11.refs_3_, ...), custom_call_target="tpu_custom_call" | custom-call | flops 8000000000 | bytes 8000000 | tf_op jit(solution)/shard_map/attn/pallas_call | solution.py:132
  111.3 4.5 %all-to-all-start.2 = ((bf16[8,192,128]{2,1,0:T(8,128)(2,1)}), bf16[8,192,128]{2,1,0:T(8,128)(2,1)S(1)}, u32[]{:S(2)}, u32[]{:S(2)}) async-start(bf16[8,192,128]{2,1,0:T(8,128)(2,1)} %attn.3), calls=%async_computation.2 | async-start | bytes 786432 | tf_op jit(solution)/shard_map/all_to_all | solution.py:382
  117.7 11.2 %all-to-all-done.2.value_ref = bf16[8,192,128]{2,1,0:T(8,128)(2,1)S(1)} async-done(((bf16[8,192,128]{2,1,0:T(8,128)(2,1)}), bf16[8,192,128]{2,1,0:T(8,128)(2,1)S(1)}, u32[]{:S(2)}, u32[]{:S(2)}) %all-to-all-start.2) | async-done | bytes 393248 | tf_op jit(solution)/shard_map/all_to_all | solution.py:382
  129.8 6.1 %proj.3 = (bf16[128,1536]{1,0:T(8,128)(2,1)}, bf16[128,1536]{1,0:T(8,128)(2,1)}) custom-call(s32[8]{0:T(128)} %get-tuple-element.35.idx_ref, bf16[8,192,128]{2,1,0:T(8,128)(2,1)} %copy-done.8, bf16[192,1536]{1,0:T(8,128)(2,1)} %refs_0_.1, bf16[192,1536]{1,0:T(8,128)(2,1)} %copy-done.12, bf16[192,1536]{1,0:T(8,128)(2,1)} %copy-done.14, ...), custom_call_target="tpu_custom_call" | custom-call | flops 8000000000 | bytes 5000000 | tf_op jit(solution)/shard_map/proj/pallas_call | solution.py:204
  135.9 1.6 collective-permute-start.19
  137.5 6.1 %proj.2 = (bf16[128,1536]{1,0:T(8,128)(2,1)}, bf16[128,1536]{1,0:T(8,128)(2,1)}) custom-call(s32[8]{0:T(128)} %get-tuple-element.35.idx_ref, bf16[8,192,128]{2,1,0:T(8,128)(2,1)} %pass_on.2.att_ref, bf16[192,1536]{1,0:T(8,128)(2,1)} %refs_0_.1, bf16[192,1536]{1,0:T(8,128)(2,1)} %copy-done.12, bf16[192,1536]{1,0:T(8,128)(2,1)} %copy-done.14, ...), custom_call_target="tpu_custom_call" | custom-call | flops 8000000000 | bytes 5000000 | tf_op jit(solution)/shard_map/proj/pallas_call | solution.py:204
  144.3 3.9 %collective-permute-done.19.value_ref = bf16[128,1536]{1,0:T(8,128)(2,1)S(1)} collective-permute-done((bf16[128,1536]{1,0:T(8,128)(2,1)}, bf16[128,1536]{1,0:T(8,128)(2,1)S(1)}, u32[]{:S(2)}, u32[]{:S(2)}) %collective-permute-start.19) | collective-permute-done | bytes 393248 | tf_op jit(solution)/shard_map/ppermute | solution.py:311
  148.9 6.5 %collective-permute-done.18.refs_0_ = bf16[128,1536]{1,0:T(8,128)(2,1)S(1)} collective-permute-done((bf16[128,1536]{1,0:T(8,128)(2,1)}, bf16[128,1536]{1,0:T(8,128)(2,1)S(1)}, u32[]{:S(2)}, u32[]{:S(2)}) %collective-permute-start.18) | collective-permute-done | bytes 393248 | tf_op jit(solution)/shard_map/ppermute | solution.py:311
  156.2 10.5 %mlp.3 = bf16[256,1536]{1,0:T(8,128)(2,1)} custom-call(bf16[128,1536]{1,0:T(8,128)(2,1)} %copy-done.7, bf16[128,1536]{1,0:T(8,128)(2,1)} %pass_on.3.refs_1_, bf16[64,2,48,1536]{3,2,1,0:T(8,128)(2,1)} %bitcast.36, bf16[64,2,48,1536]{3,2,1,0:T(8,128)(2,1)} %bitcast.37), custom_call_target="tpu_custom_call" | custom-call | flops 4831838208 | bytes 18874368 | tf_op jit(solution)/shard_map/mlp/pallas_call | solution.py:263
  167.4 10.9 %mlp.2.own_ref = f32[256,1536]{1,0:T(8,128)} custom-call(bf16[128,1536]{1,0:T(8,128)(2,1)} %get-tuple-element.27.refs_0_, bf16[128,1536]{1,0:T(8,128)(2,1)} %get-tuple-element.29.refs_1_, bf16[64,2,48,1536]{3,2,1,0:T(8,128)(2,1)} %bitcast.38, bf16[64,2,48,1536]{3,2,1,0:T(8,128)(2,1)} %bitcast.39), custom_call_target="tpu_custom_call" | custom-call | flops 4831838208 | bytes 18874368 | tf_op jit(solution)/shard_map/mlp/pallas_call | solution.py:263
  178.3 7.1 %collective-permute-done.20.back_ref = bf16[256,1536]{1,0:T(8,128)(2,1)S(1)} collective-permute-done((bf16[256,1536]{1,0:T(8,128)(2,1)}, bf16[256,1536]{1,0:T(8,128)(2,1)S(1)}, u32[]{:S(2)}, u32[]{:S(2)}) %collective-permute-start.20) | collective-permute-done | bytes 786464 | tf_op jit(solution)/shard_map/ppermute | solution.py:311
  185.4 1.4 copy-done.1
  188.5 3.1 %collective-permute-done.21 = bf16[2,32,128]{2,1,0:T(8,128)(2,1)S(1)} collective-permute-done((bf16[2,32,128]{2,1,0:T(8,128)(2,1)S(1)}, bf16[2,32,128]{2,1,0:T(8,128)(2,1)S(1)}, u32[]{:S(2)}, u32[]{:S(2)}) %collective-permute-start.21) | collective-permute-done | bytes 16416 | tf_op jit(solution)/shard_map/ppermute | solution.py:311
  (112 shorter events, 15.3 us)
Async XLA Ops:
  7.2 148.3 %all-gather.3.cloned.1.call-start = ((), (), s32[]{:S(2)}) async-start(), calls=%async_computation.3 | async-start | bytes 19169280 | tf_op jit(solution)/shard_map/all_gather | solution.py:349
  10.7 28.6 %collective-permute-start = (bf16[2,160,1536]{2,1,0:T(8,128)(2,1)S(1)}, bf16[2,160,1536]{2,1,0:T(8,128)(2,1)S(1)}, u32[]{:S(2)}, u32[]{:S(2)}) collective-permute-start(bf16[2,160,1536]{2,1,0:T(8,128)(2,1)S(1)} %maximum_maximum_fusion.refs_0_), channel_id=1, source_target_pairs={{0,6},{2,0},{4,2},{6,4},{1,7},{3,1},{5,3},{7,5},{8,14},{10,8},{12,... | collective-permute-start | bytes 2949128 | tf_op jit(solution)/shard_map/ppermute | solution.py:311
  13.8 29.5 %collective-permute-start.4 = (bf16[2,160,1536]{2,1,0:T(8,128)(2,1)S(1)}, bf16[2,160,1536]{2,1,0:T(8,128)(2,1)}, u32[]{:S(2)}, u32[]{:S(2)}) collective-permute-start(bf16[2,160,1536]{2,1,0:T(8,128)(2,1)S(1)} %maximum_maximum_fusion.refs_0_), channel_id=1, source_target_pairs={{0,2},{2,4},{4,6},{6,0},{1,3},{3,5},{5,7},{7,1},{8,10},{10,12},{12... | collective-permute-start | bytes 2949128 | tf_op jit(solution)/shard_map/ppermute | solution.py:311
  13.8 49.4 %collective-permute-start.5 = (bf16[2,160,1536]{2,1,0:T(8,128)(2,1)S(1)}, bf16[2,160,1536]{2,1,0:T(8,128)(2,1)}, u32[]{:S(2)}, u32[]{:S(2)}) collective-permute-start(bf16[2,160,1536]{2,1,0:T(8,128)(2,1)S(1)} %maximum_maximum_fusion.refs_0_), channel_id=1, source_target_pairs={{0,1},{1,0},{2,3},{3,2},{4,5},{5,4},{6,7},{7,6},{8,9},{9,8},{10,11... | collective-permute-start | bytes 2949128 | tf_op jit(solution)/shard_map/ppermute | solution.py:311
  14.8 47.3 %all-to-all-start = ((f32[64,4,128]{2,1,0:T(4,128)}), f32[64,4,128]{2,1,0:T(4,128)S(1)}, u32[]{:S(2)}, u32[]{:S(2)}) async-start(f32[64,4,128]{2,1,0:T(4,128)} %bitcast.1), calls=%async_computation | async-start | bytes 262144 | tf_op jit(solution)/shard_map/all_to_all | solution.py:358
  39.3 21.7 %collective-permute-start.1 = (bf16[160,1536]{1,0:T(8,128)(2,1)S(1)}, bf16[160,1536]{1,0:T(8,128)(2,1)}, u32[]{:S(2)}, u32[]{:S(2)}) collective-permute-start(bf16[160,1536]{1,0:T(8,128)(2,1)S(1)} %slice_bitcast_fusion.1), channel_id=1, source_target_pairs={{0,6},{2,0},{4,2},{6,4},{1,7},{3,1},{5,3},{7,5},{8,14},{10,8},{12,... | collective-permute-start | bytes 1474568 | tf_op jit(solution)/shard_map/ppermute | solution.py:311
  43.2 27.3 %collective-permute-start.7 = (bf16[2,160,1536]{2,1,0:T(8,128)(2,1)S(1)}, bf16[2,160,1536]{2,1,0:T(8,128)(2,1)}, u32[]{:S(2)}, u32[]{:S(2)}) collective-permute-start(bf16[2,160,1536]{2,1,0:T(8,128)(2,1)S(1)} %collective-permute-done.refs_2_), channel_id=1, source_target_pairs={{0,1},{1,0},{2,3},{3,2},{4,5},{5,4},{6,7},{7,6},{8,9},{9,8},{10,11... | collective-permute-start | bytes 2949128 | tf_op jit(solution)/shard_map/ppermute | solution.py:311
  43.3 27.2 %collective-permute-start.6 = (bf16[2,160,1536]{2,1,0:T(8,128)(2,1)}, bf16[2,160,1536]{2,1,0:T(8,128)(2,1)}, u32[]{:S(2)}, u32[]{:S(2)}) collective-permute-start(bf16[2,160,1536]{2,1,0:T(8,128)(2,1)} %collective-permute-done.4.refs_1_), channel_id=1, source_target_pairs={{0,1},{1,0},{2,3},{3,2},{4,5},{5,4},{6,7},{7,6},{8,9},{9,8},{10,11... | collective-permute-start | bytes 2949128 | tf_op jit(solution)/shard_map/ppermute | solution.py:311
  44.8 25.6 %collective-permute-start.11 = (bf16[160,1536]{1,0:T(8,128)(2,1)S(1)}, bf16[160,1536]{1,0:T(8,128)(2,1)}, u32[]{:S(2)}, u32[]{:S(2)}) collective-permute-start(bf16[160,1536]{1,0:T(8,128)(2,1)S(1)} %slice_bitcast_fusion), channel_id=1, source_target_pairs={{0,2},{2,4},{4,6},{6,0},{1,3},{3,5},{5,7},{7,1},{8,10},{10,12},{12... | collective-permute-start | bytes 1474568 | tf_op jit(solution)/shard_map/ppermute | solution.py:311
  63.1 23.9 %collective-permute-start.2 = (bf16[192,1536]{1,0:T(8,128)(2,1)}, bf16[192,1536]{1,0:T(8,128)(2,1)S(1)}, u32[]{:S(2)}, u32[]{:S(2)}) collective-permute-start(bf16[192,1536]{1,0:T(8,128)(2,1)} %refs_0_.1), channel_id=1, source_target_pairs={{0,2},{2,4},{4,6},{6,0},{1,3},{3,5},{5,7},{7,1},{8,10},{10,12},{12... | collective-permute-start | bytes 1769480 | tf_op jit(solution)/shard_map/ppermute | solution.py:311
  70.4 16.6 %collective-permute-start.3 = (bf16[192,1536]{1,0:T(8,128)(2,1)}, bf16[192,1536]{1,0:T(8,128)(2,1)S(1)}, u32[]{:S(2)}, u32[]{:S(2)}) collective-permute-start(bf16[192,1536]{1,0:T(8,128)(2,1)} %refs_0_.1), channel_id=1, source_target_pairs={{0,6},{2,0},{4,2},{6,4},{1,7},{3,1},{5,3},{7,5},{8,14},{10,8},{12,... | collective-permute-start | bytes 1769480 | tf_op jit(solution)/shard_map/ppermute | solution.py:311
  70.4 23.5 %collective-permute-start.12 = (bf16[160,1536]{1,0:T(8,128)(2,1)}, bf16[160,1536]{1,0:T(8,128)(2,1)}, u32[]{:S(2)}, u32[]{:S(2)}) collective-permute-start(bf16[160,1536]{1,0:T(8,128)(2,1)} %collective-permute-done.11.refs_3_), channel_id=1, source_target_pairs={{0,1},{1,0},{2,3},{3,2},{4,5},{5,4},{6,7},{7,6},{8,9},{9,8},{10,11... | collective-permute-start | bytes 1474568 | tf_op jit(solution)/shard_map/ppermute | solution.py:311
  87.9 22.7 %collective-permute-start.10 = (bf16[96,1536]{1,0:T(8,128)(2,1)S(1)}, bf16[96,1536]{1,0:T(8,128)(2,1)S(1)}, u32[]{:S(2)}, u32[]{:S(2)}) collective-permute-start(bf16[96,1536]{1,0:T(8,128)(2,1)S(1)} %slice.26), channel_id=1, source_target_pairs={{0,6},{2,0},{4,2},{6,4},{1,7},{3,1},{5,3},{7,5},{8,14},{10,8},{12,... | collective-permute-start | bytes 884744 | tf_op jit(solution)/shard_map/ppermute | solution.py:311
  88.1 22.5 %collective-permute-start.9 = (bf16[96,1536]{1,0:T(8,128)(2,1)S(1)}, bf16[96,1536]{1,0:T(8,128)(2,1)}, u32[]{:S(2)}, u32[]{:S(2)}) collective-permute-start(bf16[96,1536]{1,0:T(8,128)(2,1)S(1)} %slice.25), channel_id=1, source_target_pairs={{0,2},{2,4},{4,6},{6,0},{1,3},{3,5},{5,7},{7,1},{8,10},{10,12},{12... | collective-permute-start | bytes 884744 | tf_op jit(solution)/shard_map/ppermute | solution.py:311
  90.2 20.4 %all-to-all-start.1 = ((bf16[8,192,128]{2,1,0:T(8,128)(2,1)}), bf16[8,192,128]{2,1,0:T(8,128)(2,1)S(1)}, u32[]{:S(2)}, u32[]{:S(2)}) async-start(bf16[8,192,128]{2,1,0:T(8,128)(2,1)} %attn.2), calls=%async_computation.1 | async-start | bytes 786432 | tf_op jit(solution)/shard_map/all_to_all | solution.py:378
  111.3 17.6 %all-to-all-start.2 = ((bf16[8,192,128]{2,1,0:T(8,128)(2,1)}), bf16[8,192,128]{2,1,0:T(8,128)(2,1)S(1)}, u32[]{:S(2)}, u32[]{:S(2)}) async-start(bf16[8,192,128]{2,1,0:T(8,128)(2,1)} %attn.3), calls=%async_computation.2 | async-start | bytes 786432 | tf_op jit(solution)/shard_map/all_to_all | solution.py:382
  115.9 13.9 %collective-permute-start.13 = (bf16[192,1536]{1,0:T(8,128)(2,1)}, bf16[192,1536]{1,0:T(8,128)(2,1)}, u32[]{:S(2)}, u32[]{:S(2)}) collective-permute-start(bf16[192,1536]{1,0:T(8,128)(2,1)} %refs_0_.1), channel_id=1, source_target_pairs={{0,1},{1,0},{2,3},{3,2},{4,5},{5,4},{6,7},{7,6},{8,9},{9,8},{10,11... | collective-permute-start | bytes 1769480 | tf_op jit(solution)/shard_map/ppermute | solution.py:311
  116.4 13.4 %collective-permute-start.14 = (bf16[192,1536]{1,0:T(8,128)(2,1)S(1)}, bf16[192,1536]{1,0:T(8,128)(2,1)}, u32[]{:S(2)}, u32[]{:S(2)}) collective-permute-start(bf16[192,1536]{1,0:T(8,128)(2,1)S(1)} %copy-done.13), channel_id=1, source_target_pairs={{0,1},{1,0},{2,3},{3,2},{4,5},{5,4},{6,7},{7,6},{8,9},{9,8},{10,11... | collective-permute-start | bytes 1769480 | tf_op jit(solution)/shard_map/ppermute | solution.py:311
  116.5 13.3 %collective-permute-start.15 = (bf16[192,1536]{1,0:T(8,128)(2,1)S(1)}, bf16[192,1536]{1,0:T(8,128)(2,1)}, u32[]{:S(2)}, u32[]{:S(2)}) collective-permute-start(bf16[192,1536]{1,0:T(8,128)(2,1)S(1)} %copy-done.15), channel_id=1, source_target_pairs={{0,1},{1,0},{2,3},{3,2},{4,5},{5,4},{6,7},{7,6},{8,9},{9,8},{10,11... | collective-permute-start | bytes 1769480 | tf_op jit(solution)/shard_map/ppermute | solution.py:311
  117.1 12.6 %collective-permute-start.16 = (bf16[96,1536]{1,0:T(8,128)(2,1)}, bf16[96,1536]{1,0:T(8,128)(2,1)}, u32[]{:S(2)}, u32[]{:S(2)}) collective-permute-start(bf16[96,1536]{1,0:T(8,128)(2,1)} %collective-permute-done.9.refs_3_), channel_id=1, source_target_pairs={{0,1},{1,0},{2,3},{3,2},{4,5},{5,4},{6,7},{7,6},{8,9},{9,8},{10,11... | collective-permute-start | bytes 884744 | tf_op jit(solution)/shard_map/ppermute | solution.py:311
  117.3 12.5 %collective-permute-start.17 = (bf16[96,1536]{1,0:T(8,128)(2,1)}, bf16[96,1536]{1,0:T(8,128)(2,1)}, u32[]{:S(2)}, u32[]{:S(2)}) collective-permute-start(bf16[96,1536]{1,0:T(8,128)(2,1)} %copy-done.20), channel_id=1, source_target_pairs={{0,1},{1,0},{2,3},{3,2},{4,5},{5,4},{6,7},{7,6},{8,9},{9,8},{10,11... | collective-permute-start | bytes 884744 | tf_op jit(solution)/shard_map/ppermute | solution.py:311
  135.9 12.3 %collective-permute-start.19 = (bf16[128,1536]{1,0:T(8,128)(2,1)}, bf16[128,1536]{1,0:T(8,128)(2,1)S(1)}, u32[]{:S(2)}, u32[]{:S(2)}) collective-permute-start(bf16[128,1536]{1,0:T(8,128)(2,1)} %get-tuple-element.29.refs_1_), channel_id=1, source_target_pairs={{0,64},{64,0},{1,65},{65,1},{2,66},{66,2},{3,67},{67,3},{4,68},{68... | collective-permute-start | bytes 1179656 | tf_op jit(solution)/shard_map/ppermute | solution.py:311
  143.5 11.9 %collective-permute-start.18 = (bf16[128,1536]{1,0:T(8,128)(2,1)}, bf16[128,1536]{1,0:T(8,128)(2,1)S(1)}, u32[]{:S(2)}, u32[]{:S(2)}) collective-permute-start(bf16[128,1536]{1,0:T(8,128)(2,1)} %get-tuple-element.27.refs_0_), channel_id=1, source_target_pairs={{0,64},{64,0},{1,65},{65,1},{2,66},{66,2},{3,67},{67,3},{4,68},{68... | collective-permute-start | bytes 1179656 | tf_op jit(solution)/shard_map/ppermute | solution.py:311
  166.8 18.6 %collective-permute-start.20 = (bf16[256,1536]{1,0:T(8,128)(2,1)}, bf16[256,1536]{1,0:T(8,128)(2,1)S(1)}, u32[]{:S(2)}, u32[]{:S(2)}) collective-permute-start(bf16[256,1536]{1,0:T(8,128)(2,1)} %mlp.3), channel_id=1, source_target_pairs={{0,64},{64,0},{1,65},{65,1},{2,66},{66,2},{3,67},{67,3},{4,68},{68... | collective-permute-start | bytes 2359304 | tf_op jit(solution)/shard_map/ppermute | solution.py:311
  (23 other events, 350.2 us)
Sparse Core Ops, SparseCore 0:
  11.1 125.6 all-gather.2

commit v4 on v3

--- a/solution.py
+++ b/solution.py
@@ -346,7 +346,8 @@
     mates = [swap(block, "core") for block in pairs]
     tokens = [pairs + [far[p]] + mates + [swap(far[p], "core")] for p in range(prompts)]
 
-    weights = lax.all_gather(jnp.stack([w_up, w_down])[None], REQ + SEQ, axis=0, tiled=True)
+    up, down, _ = lax.optimization_barrier((w_up, w_down, mine))
+    weights = lax.all_gather(jnp.stack([up, down])[None], REQ + SEQ, axis=0, tiled=True)
 
     cond_act = jax.nn.silu(cond_vec[0]).astype(jnp.bfloat16)
     part = dot(cond_act, w_mod, NT)

time: 200 us -> 194 us (0.970)
  waiting for transfers between devices: 68.3 us -> 60.9 us
  starting transfers between devices: 33.4 us -> 35.9 us
    ppermute x22, waiting for transfers between devices: 57.1 us -> 51.4 us  [shifted(): lax.ppermute(value, axis, [(i, (i + by) % size) for i in range(size)])]
    ppermute x22, starting transfers between devices: 14.4 us -> 16.9 us  [shifted(): lax.ppermute(value, axis, [(i, (i + by) % size) for i in range(size)])]
    all_to_all x1, waiting for transfers between devices: 11.2 us -> 8.87 us  [local(): last = lax.all_to_all(last, SEQ, 0, 0, tiled=True)]
    unnamed x43 -> x47, local copies, waits for them, and re-layouts: 5.67 us -> 5.08 us
  transfers between devices with their start and end apart: 26 -> 26, of which waited for: 8 -> 9; matrix products, arithmetic and copies ran while one was open for 4% -> 3% of each run, Pallas kernels for 28% -> 29%
where the time goes in v4:
time: 194 us; the launch traced here: 193 us
  Pallas kernels  68.1 us (35%)
  waiting for transfers between devices  60.9 us (31%)
  starting transfers between devices  35.9 us (19%)
  between operations  14.5 us (7%)
  local copies, waits for them, and re-layouts  8.47 us (4%)
  other arithmetic  4.84 us (2%)
    ppermute x22, waiting for transfers between devices, shifted(): lax.ppermute(value, axis, [(i, (i + by) % size) for i in range(size)])  51.4 us
    pallas_call x2, Pallas kernels, attention(): pl.pallas_call(functools.partial(attn_kernel, prompt, many), out_shape=ja...  33.3 us
    pallas_call x2, Pallas kernels, mlp(): pl.pallas_call(mlp_kernel, out_shape=jax.ShapeDtypeStruct((count, width),...  21.4 us
    ppermute x22, starting transfers between devices, shifted(): lax.ppermute(value, axis, [(i, (i + by) % size) for i in range(size)])  16.9 us
    pallas_call x2, Pallas kernels, project(): pl.pallas_call(functools.partial(proj_kernel, many), out_shape=[jax.Shape...  12.4 us
    all_to_all x1, starting transfers between devices, local(): got = lax.all_to_all(part, REQ + SEQ, 0, 0, tiled=True)  10.8 us
    all_to_all x1, waiting for transfers between devices, local(): last = lax.all_to_all(last, SEQ, 0, 0, tiled=True)  8.87 us
    unnamed x47, local copies, waits for them, and re-layouts  5.08 us
  transfers between devices with their start and end apart: 26, of which 9 were waited for; matrix products, arithmetic and copies ran while one was open for 3% of the time, Pallas kernels for 29%

profile of v4, /device:TPU:70, one launch (start us, length us, event | category | flops | bytes accessed | tf_op | source)
XLA Modules:
  0.0 192.9 jit_solution(3666975388099001815)
XLA Ops:
  7.3 1.6 maximum_maximum_fusion.refs_0_
  9.9 3.1 %collective-permute-start = (bf16[2,160,1536]{2,1,0:T(8,128)(2,1)S(1)}, bf16[2,160,1536]{2,1,0:T(8,128)(2,1)S(1)}, u32[]{:S(2)}, u32[]{:S(2)}) collective-permute-start(bf16[2,160,1536]{2,1,0:T(8,128)(2,1)S(1)} %maximum_maximum_fusion.refs_0_), channel_id=1, source_target_pairs={{0,6},{2,0},{4,2},{6,4},{1,7},{3,1},{5,3},{7,5},{8,14},{10,8},{12,... | collective-permute-start | bytes 2949128 | tf_op jit(solution)/shard_map/ppermute | solution.py:311
  14.0 10.8 %all-to-all-start = ((f32[64,4,128]{2,1,0:T(4,128)}), f32[64,4,128]{2,1,0:T(4,128)S(1)}, u32[]{:S(2)}, u32[]{:S(2)}) async-start(f32[64,4,128]{2,1,0:T(4,128)} %bitcast.1), calls=%async_computation | async-start | bytes 262144 | tf_op jit(solution)/shard_map/all_to_all | solution.py:359
  25.4 13.1 %collective-permute-done.refs_2_ = bf16[2,160,1536]{2,1,0:T(8,128)(2,1)S(1)} collective-permute-done((bf16[2,160,1536]{2,1,0:T(8,128)(2,1)S(1)}, bf16[2,160,1536]{2,1,0:T(8,128)(2,1)S(1)}, u32[]{:S(2)}, u32[]{:S(2)}) %collective-permute-start) | collective-permute-done | bytes 983072 | tf_op jit(solution)/shard_map/ppermute | solution.py:311
  38.5 3.8 %collective-permute-start.1 = (bf16[160,1536]{1,0:T(8,128)(2,1)S(1)}, bf16[160,1536]{1,0:T(8,128)(2,1)}, u32[]{:S(2)}, u32[]{:S(2)}) collective-permute-start(bf16[160,1536]{1,0:T(8,128)(2,1)S(1)} %slice_bitcast_fusion.1), channel_id=1, source_target_pairs={{0,6},{2,0},{4,2},{6,4},{1,7},{3,1},{5,3},{7,5},{8,14},{10,8},{12,... | collective-permute-start | bytes 1474568 | tf_op jit(solution)/shard_map/ppermute | solution.py:311
  44.1 14.6 %collective-permute-done.1.refs_3_ = bf16[160,1536]{1,0:T(8,128)(2,1)} collective-permute-done((bf16[160,1536]{1,0:T(8,128)(2,1)S(1)}, bf16[160,1536]{1,0:T(8,128)(2,1)}, u32[]{:S(2)}, u32[]{:S(2)}) %collective-permute-start.1) | collective-permute-done | bytes 491552 | tf_op jit(solution)/shard_map/ppermute | solution.py:311
  60.8 7.6 %collective-permute-done.11.refs_3_ = bf16[160,1536]{1,0:T(8,128)(2,1)} collective-permute-done((bf16[160,1536]{1,0:T(8,128)(2,1)S(1)}, bf16[160,1536]{1,0:T(8,128)(2,1)}, u32[]{:S(2)}, u32[]{:S(2)}) %collective-permute-start.11) | collective-permute-done | bytes 491552 | tf_op jit(solution)/shard_map/ppermute | solution.py:311
  68.5 16.6 %attn.2 = bf16[8,192,128]{2,1,0:T(8,128)(2,1)} custom-call(s32[8]{0:T(128)} %get-tuple-element.39.idx_ref, bf16[2,160,1536]{2,1,0:T(8,128)(2,1)} %copy-done.5, bf16[2,160,1536]{2,1,0:T(8,128)(2,1)} %collective-permute-done.4.refs_1_, bf16[2,160,1536]{2,1,0:T(8,128)(2,1)} %copy-done.10, bf16[160,1536]{1,0:T(8,128)(2,1)} %collective-permute-done.1.refs_3_, ...), custom_call_target="tpu_custom_call" | custom-call | flops 8000000000 | bytes 8000000 | tf_op jit(solution)/shard_map/attn/pallas_call | solution.py:132
  86.1 2.1 %collective-permute-start.9 = (bf16[96,1536]{1,0:T(8,128)(2,1)S(1)}, bf16[96,1536]{1,0:T(8,128)(2,1)}, u32[]{:S(2)}, u32[]{:S(2)}) collective-permute-start(bf16[96,1536]{1,0:T(8,128)(2,1)S(1)} %slice.25), channel_id=1, source_target_pairs={{0,2},{2,4},{4,6},{6,0},{1,3},{3,5},{5,7},{7,1},{8,10},{10,12},{12... | collective-permute-start | bytes 884744 | tf_op jit(solution)/shard_map/ppermute | solution.py:311
  88.2 3.6 %all-to-all-start.1 = ((bf16[8,192,128]{2,1,0:T(8,128)(2,1)}), bf16[8,192,128]{2,1,0:T(8,128)(2,1)S(1)}, u32[]{:S(2)}, u32[]{:S(2)}) async-start(bf16[8,192,128]{2,1,0:T(8,128)(2,1)} %attn.2), calls=%async_computation.1 | async-start | bytes 786432 | tf_op jit(solution)/shard_map/all_to_all | solution.py:379
  91.8 16.7 %attn.3 = bf16[8,192,128]{2,1,0:T(8,128)(2,1)} custom-call(s32[8]{0:T(128)} %get-tuple-element.39.idx_ref, bf16[2,160,1536]{2,1,0:T(8,128)(2,1)} %copy-done.5, bf16[2,160,1536]{2,1,0:T(8,128)(2,1)} %collective-permute-done.4.refs_1_, bf16[2,160,1536]{2,1,0:T(8,128)(2,1)} %copy-done.10, bf16[160,1536]{1,0:T(8,128)(2,1)} %collective-permute-done.11.refs_3_, ...), custom_call_target="tpu_custom_call" | custom-call | flops 8000000000 | bytes 8000000 | tf_op jit(solution)/shard_map/attn/pallas_call | solution.py:132
  109.3 4.5 %all-to-all-start.2 = ((bf16[8,192,128]{2,1,0:T(8,128)(2,1)}), bf16[8,192,128]{2,1,0:T(8,128)(2,1)S(1)}, u32[]{:S(2)}, u32[]{:S(2)}) async-start(bf16[8,192,128]{2,1,0:T(8,128)(2,1)} %attn.3), calls=%async_computation.2 | async-start | bytes 786432 | tf_op jit(solution)/shard_map/all_to_all | solution.py:383
  115.7 8.9 %all-to-all-done.2.value_ref = bf16[8,192,128]{2,1,0:T(8,128)(2,1)S(1)} async-done(((bf16[8,192,128]{2,1,0:T(8,128)(2,1)}), bf16[8,192,128]{2,1,0:T(8,128)(2,1)S(1)}, u32[]{:S(2)}, u32[]{:S(2)}) %all-to-all-start.2) | async-done | bytes 393248 | tf_op jit(solution)/shard_map/all_to_all | solution.py:383
  125.4 6.4 %proj.3 = (bf16[128,1536]{1,0:T(8,128)(2,1)}, bf16[128,1536]{1,0:T(8,128)(2,1)}) custom-call(s32[8]{0:T(128)} %get-tuple-element.39.idx_ref, bf16[8,192,128]{2,1,0:T(8,128)(2,1)} %copy-done.8, bf16[192,1536]{1,0:T(8,128)(2,1)} %refs_0_.1, bf16[192,1536]{1,0:T(8,128)(2,1)} %copy-done.12, bf16[192,1536]{1,0:T(8,128)(2,1)} %copy-done.14, ...), custom_call_target="tpu_custom_call" | custom-call | flops 8000000000 | bytes 5000000 | tf_op jit(solution)/shard_map/proj/pallas_call | solution.py:204
  131.7 2.1 %collective-permute-start.19 = (bf16[128,1536]{1,0:T(8,128)(2,1)}, bf16[128,1536]{1,0:T(8,128)(2,1)S(1)}, u32[]{:S(2)}, u32[]{:S(2)}) collective-permute-start(bf16[128,1536]{1,0:T(8,128)(2,1)} %get-tuple-element.31.refs_1_), channel_id=1, source_target_pairs={{0,64},{64,0},{1,65},{65,1},{2,66},{66,2},{3,67},{67,3},{4,68},{68... | collective-permute-start | bytes 1179656 | tf_op jit(solution)/shard_map/ppermute | solution.py:311
  133.9 6.1 %proj.2 = (bf16[128,1536]{1,0:T(8,128)(2,1)}, bf16[128,1536]{1,0:T(8,128)(2,1)}) custom-call(s32[8]{0:T(128)} %get-tuple-element.39.idx_ref, bf16[8,192,128]{2,1,0:T(8,128)(2,1)} %pass_on.2.att_ref, bf16[192,1536]{1,0:T(8,128)(2,1)} %refs_0_.1, bf16[192,1536]{1,0:T(8,128)(2,1)} %copy-done.12, bf16[192,1536]{1,0:T(8,128)(2,1)} %copy-done.14, ...), custom_call_target="tpu_custom_call" | custom-call | flops 8000000000 | bytes 5000000 | tf_op jit(solution)/shard_map/proj/pallas_call | solution.py:204
  140.3 3.1 %collective-permute-done.19.value_ref = bf16[128,1536]{1,0:T(8,128)(2,1)S(1)} collective-permute-done((bf16[128,1536]{1,0:T(8,128)(2,1)}, bf16[128,1536]{1,0:T(8,128)(2,1)S(1)}, u32[]{:S(2)}, u32[]{:S(2)}) %collective-permute-start.19) | collective-permute-done | bytes 393248 | tf_op jit(solution)/shard_map/ppermute | solution.py:311
  144.1 6.1 %collective-permute-done.18.refs_0_ = bf16[128,1536]{1,0:T(8,128)(2,1)S(1)} collective-permute-done((bf16[128,1536]{1,0:T(8,128)(2,1)}, bf16[128,1536]{1,0:T(8,128)(2,1)S(1)}, u32[]{:S(2)}, u32[]{:S(2)}) %collective-permute-start.18) | collective-permute-done | bytes 393248 | tf_op jit(solution)/shard_map/ppermute | solution.py:311
  151.0 10.5 %mlp.3 = bf16[256,1536]{1,0:T(8,128)(2,1)} custom-call(bf16[128,1536]{1,0:T(8,128)(2,1)} %copy-done.7, bf16[128,1536]{1,0:T(8,128)(2,1)} %pass_on.3.refs_1_, bf16[64,2,48,1536]{3,2,1,0:T(8,128)(2,1)} %bitcast.36, bf16[64,2,48,1536]{3,2,1,0:T(8,128)(2,1)} %bitcast.37), custom_call_target="tpu_custom_call" | custom-call | flops 4831838208 | bytes 18874368 | tf_op jit(solution)/shard_map/mlp/pallas_call | solution.py:263
  161.5 1.7 collective-permute-start.20
  163.6 10.9 %mlp.2.own_ref = f32[256,1536]{1,0:T(8,128)} custom-call(bf16[128,1536]{1,0:T(8,128)(2,1)} %get-tuple-element.29.refs_0_, bf16[128,1536]{1,0:T(8,128)(2,1)} %get-tuple-element.31.refs_1_, bf16[64,2,48,1536]{3,2,1,0:T(8,128)(2,1)} %bitcast.38, bf16[64,2,48,1536]{3,2,1,0:T(8,128)(2,1)} %bitcast.39), custom_call_target="tpu_custom_call" | custom-call | flops 4831838208 | bytes 18874368 | tf_op jit(solution)/shard_map/mlp/pallas_call | solution.py:263
  174.5 4.8 %collective-permute-done.20.back_ref = bf16[256,1536]{1,0:T(8,128)(2,1)S(1)} collective-permute-done((bf16[256,1536]{1,0:T(8,128)(2,1)}, bf16[256,1536]{1,0:T(8,128)(2,1)S(1)}, u32[]{:S(2)}, u32[]{:S(2)}) %collective-permute-start.20) | collective-permute-done | bytes 786464 | tf_op jit(solution)/shard_map/ppermute | solution.py:311
  181.6 1.7 collective-permute-start.21
  183.3 2.1 %collective-permute-done.21 = bf16[2,32,128]{2,1,0:T(8,128)(2,1)S(1)} collective-permute-done((bf16[2,32,128]{2,1,0:T(8,128)(2,1)S(1)}, bf16[2,32,128]{2,1,0:T(8,128)(2,1)S(1)}, u32[]{:S(2)}, u32[]{:S(2)}) %collective-permute-start.21) | collective-permute-done | bytes 16416 | tf_op jit(solution)/shard_map/ppermute | solution.py:311
  (116 shorter events, 16.0 us)
Async XLA Ops:
  7.2 143.0 %all-gather.3.cloned.1.call-start = ((), (), s32[]{:S(2)}) async-start(), calls=%async_computation.3 | async-start | bytes 19169280 | tf_op jit(solution)/shard_map/all_gather | solution.py:350
  9.9 28.6 %collective-permute-start = (bf16[2,160,1536]{2,1,0:T(8,128)(2,1)S(1)}, bf16[2,160,1536]{2,1,0:T(8,128)(2,1)S(1)}, u32[]{:S(2)}, u32[]{:S(2)}) collective-permute-start(bf16[2,160,1536]{2,1,0:T(8,128)(2,1)S(1)} %maximum_maximum_fusion.refs_0_), channel_id=1, source_target_pairs={{0,6},{2,0},{4,2},{6,4},{1,7},{3,1},{5,3},{7,5},{8,14},{10,8},{12,... | collective-permute-start | bytes 2949128 | tf_op jit(solution)/shard_map/ppermute | solution.py:311
  12.9 29.5 %collective-permute-start.4 = (bf16[2,160,1536]{2,1,0:T(8,128)(2,1)S(1)}, bf16[2,160,1536]{2,1,0:T(8,128)(2,1)}, u32[]{:S(2)}, u32[]{:S(2)}) collective-permute-start(bf16[2,160,1536]{2,1,0:T(8,128)(2,1)S(1)} %maximum_maximum_fusion.refs_0_), channel_id=1, source_target_pairs={{0,2},{2,4},{4,6},{6,0},{1,3},{3,5},{5,7},{7,1},{8,10},{10,12},{12... | collective-permute-start | bytes 2949128 | tf_op jit(solution)/shard_map/ppermute | solution.py:311
  12.9 47.8 %collective-permute-start.5 = (bf16[2,160,1536]{2,1,0:T(8,128)(2,1)S(1)}, bf16[2,160,1536]{2,1,0:T(8,128)(2,1)}, u32[]{:S(2)}, u32[]{:S(2)}) collective-permute-start(bf16[2,160,1536]{2,1,0:T(8,128)(2,1)S(1)} %maximum_maximum_fusion.refs_0_), channel_id=1, source_target_pairs={{0,1},{1,0},{2,3},{3,2},{4,5},{5,4},{6,7},{7,6},{8,9},{9,8},{10,11... | collective-permute-start | bytes 2949128 | tf_op jit(solution)/shard_map/ppermute | solution.py:311
  14.0 45.8 %all-to-all-start = ((f32[64,4,128]{2,1,0:T(4,128)}), f32[64,4,128]{2,1,0:T(4,128)S(1)}, u32[]{:S(2)}, u32[]{:S(2)}) async-start(f32[64,4,128]{2,1,0:T(4,128)} %bitcast.1), calls=%async_computation | async-start | bytes 262144 | tf_op jit(solution)/shard_map/all_to_all | solution.py:359
  38.5 20.2 %collective-permute-start.1 = (bf16[160,1536]{1,0:T(8,128)(2,1)S(1)}, bf16[160,1536]{1,0:T(8,128)(2,1)}, u32[]{:S(2)}, u32[]{:S(2)}) collective-permute-start(bf16[160,1536]{1,0:T(8,128)(2,1)S(1)} %slice_bitcast_fusion.1), channel_id=1, source_target_pairs={{0,6},{2,0},{4,2},{6,4},{1,7},{3,1},{5,3},{7,5},{8,14},{10,8},{12,... | collective-permute-start | bytes 1474568 | tf_op jit(solution)/shard_map/ppermute | solution.py:311
  42.3 26.1 %collective-permute-start.7 = (bf16[2,160,1536]{2,1,0:T(8,128)(2,1)S(1)}, bf16[2,160,1536]{2,1,0:T(8,128)(2,1)}, u32[]{:S(2)}, u32[]{:S(2)}) collective-permute-start(bf16[2,160,1536]{2,1,0:T(8,128)(2,1)S(1)} %collective-permute-done.refs_2_), channel_id=1, source_target_pairs={{0,1},{1,0},{2,3},{3,2},{4,5},{5,4},{6,7},{7,6},{8,9},{9,8},{10,11... | collective-permute-start | bytes 2949128 | tf_op jit(solution)/shard_map/ppermute | solution.py:311
  42.4 26.0 %collective-permute-start.6 = (bf16[2,160,1536]{2,1,0:T(8,128)(2,1)}, bf16[2,160,1536]{2,1,0:T(8,128)(2,1)}, u32[]{:S(2)}, u32[]{:S(2)}) collective-permute-start(bf16[2,160,1536]{2,1,0:T(8,128)(2,1)} %collective-permute-done.4.refs_1_), channel_id=1, source_target_pairs={{0,1},{1,0},{2,3},{3,2},{4,5},{5,4},{6,7},{7,6},{8,9},{9,8},{10,11... | collective-permute-start | bytes 2949128 | tf_op jit(solution)/shard_map/ppermute | solution.py:311
  44.0 24.4 %collective-permute-start.11 = (bf16[160,1536]{1,0:T(8,128)(2,1)S(1)}, bf16[160,1536]{1,0:T(8,128)(2,1)}, u32[]{:S(2)}, u32[]{:S(2)}) collective-permute-start(bf16[160,1536]{1,0:T(8,128)(2,1)S(1)} %slice_bitcast_fusion), channel_id=1, source_target_pairs={{0,2},{2,4},{4,6},{6,0},{1,3},{3,5},{5,7},{7,1},{8,10},{10,12},{12... | collective-permute-start | bytes 1474568 | tf_op jit(solution)/shard_map/ppermute | solution.py:311
  60.8 24.3 %collective-permute-start.2 = (bf16[192,1536]{1,0:T(8,128)(2,1)}, bf16[192,1536]{1,0:T(8,128)(2,1)S(1)}, u32[]{:S(2)}, u32[]{:S(2)}) collective-permute-start(bf16[192,1536]{1,0:T(8,128)(2,1)} %refs_0_.1), channel_id=1, source_target_pairs={{0,2},{2,4},{4,6},{6,0},{1,3},{3,5},{5,7},{7,1},{8,10},{10,12},{12... | collective-permute-start | bytes 1769480 | tf_op jit(solution)/shard_map/ppermute | solution.py:311
  68.4 16.6 %collective-permute-start.3 = (bf16[192,1536]{1,0:T(8,128)(2,1)}, bf16[192,1536]{1,0:T(8,128)(2,1)S(1)}, u32[]{:S(2)}, u32[]{:S(2)}) collective-permute-start(bf16[192,1536]{1,0:T(8,128)(2,1)} %refs_0_.1), channel_id=1, source_target_pairs={{0,6},{2,0},{4,2},{6,4},{1,7},{3,1},{5,3},{7,5},{8,14},{10,8},{12,... | collective-permute-start | bytes 1769480 | tf_op jit(solution)/shard_map/ppermute | solution.py:311
  68.4 23.4 %collective-permute-start.12 = (bf16[160,1536]{1,0:T(8,128)(2,1)}, bf16[160,1536]{1,0:T(8,128)(2,1)}, u32[]{:S(2)}, u32[]{:S(2)}) collective-permute-start(bf16[160,1536]{1,0:T(8,128)(2,1)} %collective-permute-done.11.refs_3_), channel_id=1, source_target_pairs={{0,1},{1,0},{2,3},{3,2},{4,5},{5,4},{6,7},{7,6},{8,9},{9,8},{10,11... | collective-permute-start | bytes 1474568 | tf_op jit(solution)/shard_map/ppermute | solution.py:311
  85.9 22.7 %collective-permute-start.10 = (bf16[96,1536]{1,0:T(8,128)(2,1)S(1)}, bf16[96,1536]{1,0:T(8,128)(2,1)S(1)}, u32[]{:S(2)}, u32[]{:S(2)}) collective-permute-start(bf16[96,1536]{1,0:T(8,128)(2,1)S(1)} %slice.26), channel_id=1, source_target_pairs={{0,6},{2,0},{4,2},{6,4},{1,7},{3,1},{5,3},{7,5},{8,14},{10,8},{12,... | collective-permute-start | bytes 884744 | tf_op jit(solution)/shard_map/ppermute | solution.py:311
  86.1 22.5 %collective-permute-start.9 = (bf16[96,1536]{1,0:T(8,128)(2,1)S(1)}, bf16[96,1536]{1,0:T(8,128)(2,1)}, u32[]{:S(2)}, u32[]{:S(2)}) collective-permute-start(bf16[96,1536]{1,0:T(8,128)(2,1)S(1)} %slice.25), channel_id=1, source_target_pairs={{0,2},{2,4},{4,6},{6,0},{1,3},{3,5},{5,7},{7,1},{8,10},{10,12},{12... | collective-permute-start | bytes 884744 | tf_op jit(solution)/shard_map/ppermute | solution.py:311
  88.2 21.0 %all-to-all-start.1 = ((bf16[8,192,128]{2,1,0:T(8,128)(2,1)}), bf16[8,192,128]{2,1,0:T(8,128)(2,1)S(1)}, u32[]{:S(2)}, u32[]{:S(2)}) async-start(bf16[8,192,128]{2,1,0:T(8,128)(2,1)} %attn.2), calls=%async_computation.1 | async-start | bytes 786432 | tf_op jit(solution)/shard_map/all_to_all | solution.py:379
  109.3 15.2 %all-to-all-start.2 = ((bf16[8,192,128]{2,1,0:T(8,128)(2,1)}), bf16[8,192,128]{2,1,0:T(8,128)(2,1)S(1)}, u32[]{:S(2)}, u32[]{:S(2)}) async-start(bf16[8,192,128]{2,1,0:T(8,128)(2,1)} %attn.3), calls=%async_computation.2 | async-start | bytes 786432 | tf_op jit(solution)/shard_map/all_to_all | solution.py:383
  113.8 11.5 %collective-permute-start.13 = (bf16[192,1536]{1,0:T(8,128)(2,1)}, bf16[192,1536]{1,0:T(8,128)(2,1)}, u32[]{:S(2)}, u32[]{:S(2)}) collective-permute-start(bf16[192,1536]{1,0:T(8,128)(2,1)} %refs_0_.1), channel_id=1, source_target_pairs={{0,1},{1,0},{2,3},{3,2},{4,5},{5,4},{6,7},{7,6},{8,9},{9,8},{10,11... | collective-permute-start | bytes 1769480 | tf_op jit(solution)/shard_map/ppermute | solution.py:311
  114.3 11.0 %collective-permute-start.14 = (bf16[192,1536]{1,0:T(8,128)(2,1)S(1)}, bf16[192,1536]{1,0:T(8,128)(2,1)}, u32[]{:S(2)}, u32[]{:S(2)}) collective-permute-start(bf16[192,1536]{1,0:T(8,128)(2,1)S(1)} %copy-done.13), channel_id=1, source_target_pairs={{0,1},{1,0},{2,3},{3,2},{4,5},{5,4},{6,7},{7,6},{8,9},{9,8},{10,11... | collective-permute-start | bytes 1769480 | tf_op jit(solution)/shard_map/ppermute | solution.py:311
  114.4 10.9 %collective-permute-start.15 = (bf16[192,1536]{1,0:T(8,128)(2,1)S(1)}, bf16[192,1536]{1,0:T(8,128)(2,1)}, u32[]{:S(2)}, u32[]{:S(2)}) collective-permute-start(bf16[192,1536]{1,0:T(8,128)(2,1)S(1)} %copy-done.15), channel_id=1, source_target_pairs={{0,1},{1,0},{2,3},{3,2},{4,5},{5,4},{6,7},{7,6},{8,9},{9,8},{10,11... | collective-permute-start | bytes 1769480 | tf_op jit(solution)/shard_map/ppermute | solution.py:311
  115.1 10.3 %collective-permute-start.16 = (bf16[96,1536]{1,0:T(8,128)(2,1)}, bf16[96,1536]{1,0:T(8,128)(2,1)}, u32[]{:S(2)}, u32[]{:S(2)}) collective-permute-start(bf16[96,1536]{1,0:T(8,128)(2,1)} %collective-permute-done.9.refs_3_), channel_id=1, source_target_pairs={{0,1},{1,0},{2,3},{3,2},{4,5},{5,4},{6,7},{7,6},{8,9},{9,8},{10,11... | collective-permute-start | bytes 884744 | tf_op jit(solution)/shard_map/ppermute | solution.py:311
  115.2 10.1 %collective-permute-start.17 = (bf16[96,1536]{1,0:T(8,128)(2,1)}, bf16[96,1536]{1,0:T(8,128)(2,1)}, u32[]{:S(2)}, u32[]{:S(2)}) collective-permute-start(bf16[96,1536]{1,0:T(8,128)(2,1)} %copy-done.22), channel_id=1, source_target_pairs={{0,1},{1,0},{2,3},{3,2},{4,5},{5,4},{6,7},{7,6},{8,9},{9,8},{10,11... | collective-permute-start | bytes 884744 | tf_op jit(solution)/shard_map/ppermute | solution.py:311
  131.7 11.6 %collective-permute-start.19 = (bf16[128,1536]{1,0:T(8,128)(2,1)}, bf16[128,1536]{1,0:T(8,128)(2,1)S(1)}, u32[]{:S(2)}, u32[]{:S(2)}) collective-permute-start(bf16[128,1536]{1,0:T(8,128)(2,1)} %get-tuple-element.31.refs_1_), channel_id=1, source_target_pairs={{0,64},{64,0},{1,65},{65,1},{2,66},{66,2},{3,67},{67,3},{4,68},{68... | collective-permute-start | bytes 1179656 | tf_op jit(solution)/shard_map/ppermute | solution.py:311
  139.9 10.3 %collective-permute-start.18 = (bf16[128,1536]{1,0:T(8,128)(2,1)}, bf16[128,1536]{1,0:T(8,128)(2,1)S(1)}, u32[]{:S(2)}, u32[]{:S(2)}) collective-permute-start(bf16[128,1536]{1,0:T(8,128)(2,1)} %get-tuple-element.29.refs_0_), channel_id=1, source_target_pairs={{0,64},{64,0},{1,65},{65,1},{2,66},{66,2},{3,67},{67,3},{4,68},{68... | collective-permute-start | bytes 1179656 | tf_op jit(solution)/shard_map/ppermute | solution.py:311
  161.5 17.7 %collective-permute-start.20 = (bf16[256,1536]{1,0:T(8,128)(2,1)}, bf16[256,1536]{1,0:T(8,128)(2,1)S(1)}, u32[]{:S(2)}, u32[]{:S(2)}) collective-permute-start(bf16[256,1536]{1,0:T(8,128)(2,1)} %mlp.3), channel_id=1, source_target_pairs={{0,64},{64,0},{1,65},{65,1},{2,66},{66,2},{3,67},{67,3},{4,68},{68... | collective-permute-start | bytes 2359304 | tf_op jit(solution)/shard_map/ppermute | solution.py:311
  (25 other events, 319.8 us)
Sparse Core Ops, SparseCore 0:
  11.1 123.7 all-gather.2
